TPU v7x, 32 devices: a whole 2x2x4 slice. The times are simulated.
32 devices in a mesh: groups: 2 (over x), tm: 16 (over z, y, core).
Axes of the slice: x: 2, y: 2, z: 4, core: 2. Of those that a mesh axis runs over, the one named last changes fastest.
Arguments:
- strain: bfloat16 [256, 48, 12032], P(('groups', 'tm')), parts along dimension 0
- bin_labels: int32 [256, 3], P(('groups', 'tm')), parts along dimension 0, may hold values from 0 to 7, as said below
- influence: bfloat16 [2048, 48], replicated, may hold values from -0.875 to 0.875
Outputs:
- damage_by_bin: float32 [256, 2048], P('groups', 'tm'), parts along dimension 0
- total_damage: float32 [4096], P(('groups', 'tm')), parts along dimension 0
There are 2 independent parts, one for each index of `groups`. A program takes and returns all parts, laid end to end along the dimension named above; an argument that names none is the same for every part. Nothing has to cross between parts.
Inputs may be any that keep to these rules, and one draw needn't show every extreme that they name: `bin_labels`: columns are wind speed (below 8), direction (below 8) and yaw (below 2); every combination of the three is named by at least one block.
All inputs are finite; a program needn't handle non-finite values.
Results may differ from a plain program's by a relative error of at most 0.00059.
Values may be sent and summed in bfloat16 or wider, within the bound.
No kernel may reach another device: no remote copies, remote signals or barrier semaphores. Data moves between devices by JAX's collectives and lax.ppermute only.
A program may use at most 128 MiB of HBM per device.

v0:
```python
import math

import jax
import jax.numpy as jnp
from jax import lax
from jax.sharding import PartitionSpec as P

SEGLEN = 128
NSEG = 187
NDIR = 8
NYAW = 2
NBIN = 128


def build_table():
    positions = jnp.arange(SEGLEN, dtype=jnp.int32)
    harmonic = jnp.arange(1, SEGLEN // 2 + 1, dtype=jnp.int32)
    phase = (positions[:, None] * harmonic[None, :] % SEGLEN).astype(jnp.float32) * (
        2.0 * math.pi / SEGLEN
    )
    window = 0.5 - 0.5 * jnp.cos(positions.astype(jnp.float32) * (2.0 * math.pi / SEGLEN))
    full_table = jnp.concatenate(
        [window[:, None] * jnp.cos(phase), window[:, None] * jnp.sin(phase)], axis=1
    ).astype(jnp.bfloat16)
    half_len = SEGLEN // 2
    return jnp.concatenate([full_table[:half_len], full_table[half_len:]], axis=1)


def block_spectra(one_block, dft_table):
    channels = one_block.shape[0]
    half_len = SEGLEN // 2
    pieces = one_block.reshape(channels, NSEG + 1, half_len)
    product = jnp.einsum("csn,nk->kcs", pieces, dft_table, preferred_element_type=jnp.float32)
    segments = (product[:SEGLEN, :, :-1] + product[SEGLEN:, :, 1:]).astype(jnp.bfloat16)
    cross = jnp.einsum("gcs,gds->gcd", segments, segments, preferred_element_type=jnp.float32)
    cospec = (cross[:half_len] + cross[half_len:]) * (8.0 / (3.0 * SEGLEN * NSEG))
    return cospec.reshape(-1).astype(jnp.bfloat16)


def spectral_moments(stress, frequency):
    moment_zero = jnp.sum(stress, axis=0) / SEGLEN
    moment_one = jnp.sum(frequency[:, None] * stress, axis=0) / SEGLEN
    moment_two = jnp.sum(frequency[:, None] ** 2 * stress, axis=0) / SEGLEN
    moment_four = jnp.sum(frequency[:, None] ** 4 * stress, axis=0) / SEGLEN
    return jnp.stack([moment_zero, moment_one, moment_two, moment_four], axis=0)


def dirlik(moment_zero, moment_one, moment_two, moment_four):
    spread_ratio = moment_two / jnp.sqrt(moment_zero * moment_four)
    mean_freq = moment_one / moment_zero * jnp.sqrt(moment_two / moment_four)
    d_one = 2.0 * (mean_freq - spread_ratio**2) / (1.0 + spread_ratio**2)
    shared = 1.0 - spread_ratio - d_one + d_one**2
    r_ratio = (spread_ratio - mean_freq - d_one**2) / shared
    d_two = shared / (1.0 - r_ratio)
    d_three = 1.0 - d_one - d_two
    q_factor = 1.25 * (spread_ratio - d_three - d_two * r_ratio) / d_one
    peak_rate = jnp.sqrt(moment_four / moment_two)
    bracket = 6.0 * d_one * q_factor**3 + 2.8284271247 * 1.3293403882 * (
        jnp.abs(r_ratio) ** 3 * d_two + d_three
    )
    return peak_rate * (2.0 * jnp.sqrt(moment_zero)) ** 3 * bracket


def per_device(strain, bin_labels, influence):
    channels = influence.shape[1]
    hotspots = influence.shape[0]
    freq_count = SEGLEN // 2
    dft_table = build_table()
    cospec = lax.map(lambda one_block: block_spectra(one_block, dft_table), strain)
    all_labels = lax.all_gather(bin_labels, "tm", axis=0, tiled=True)
    total_blocks = all_labels.shape[0]
    bin_index = (all_labels[:, 0] * NDIR + all_labels[:, 1]) * NYAW + all_labels[:, 2]
    onehot = (bin_index[None, :] == jnp.arange(NBIN, dtype=jnp.int32)[:, None]).astype(jnp.bfloat16)
    count = jnp.sum(onehot.astype(jnp.float32), axis=1)
    weights_f32 = influence.astype(jnp.float32)
    weights_cols = weights_f32.T
    frequency = jnp.arange(1, freq_count + 1, dtype=jnp.int32).astype(jnp.float32) / SEGLEN
    contract_channel = (((1,), (1,)), ((), ()))
    entry_slices = lax.all_to_all(cospec, "tm", split_axis=1, concat_axis=0, tiled=True)
    bin_sums = jnp.dot(onehot, entry_slices, preferred_element_type=jnp.float32)
    mean_cospec = bin_sums / count[:, None]
    owned_bins = lax.all_to_all(mean_cospec, "tm", split_axis=0, concat_axis=1, tiled=True)

    def bin_damage(flat_mean):
        product = lax.dot_general(
            flat_mean.reshape(freq_count * channels, channels),
            weights_f32,
            contract_channel,
            precision=lax.Precision.HIGHEST,
        )
        stress = jnp.sum(
            product.reshape(freq_count, channels, hotspots) * weights_cols[None], axis=1
        )
        moments = spectral_moments(stress, frequency)
        return dirlik(moments[0], moments[1], moments[2], moments[3])

    owned_damage = lax.map(bin_damage, owned_bins)
    damage_by_bin = lax.all_to_all(owned_damage, "tm", split_axis=1, concat_axis=0, tiled=True)
    total_damage = jnp.sum(count[:, None] / total_blocks * damage_by_bin, axis=0)
    return (damage_by_bin, total_damage)


def solution(mesh):
    placed = (P(("groups", "tm"), None, None), P(("groups", "tm"), None), P())
    return jax.shard_map(
        per_device,
        mesh=mesh,
        in_specs=placed,
        out_specs=(P("groups", "tm"), P(("groups", "tm"))),
        check_vma=False,
    )
```

profile of v0, /device:TPU:0, one launch (start us, length us, event | category | flops | bytes accessed | tf_op | source)
XLA Modules:
  0.0 670.2 jit_solution(9552309349621265536)
XLA Ops:
  1.1 208.0 %while.23 = (s32[]{:T(128)}, bf16[8,147456]{1,0:T(8,128)(2,1)}, bf16[8,48,12032]{2,1,0:T(8,128)(2,1)}, bf16[64,256]{1,0:T(8,128)(2,1)S(1)}, s32[]{:T(128)}, /*index=5*/s32[]{:T(128)}) while((s32[]{:T(128)}, bf16[8,147456]{1,0:T(8,128)(2,1)}, bf16[8,48,12032]{2,1,0:T(8,128)(2,1)}, bf16[64,256]{1,0:T(8,128)(2,1)S(1)}, s32[]{:T(128)}, ...), condition=%wide.region_1.2_spmd, body=%wide.region_0.1_spmd.sunk | while | flops 408735744 | bytes 37265484 | solution.py:69
  2.5 2.6 reshape.309
  5.0 1.9 convolution_bitcast_fusion.2
  7.0 1.9 fusion.48
  8.9 4.6 copy.33
  15.7 11.5 %dynamic_update_slice.13 = bf16[8,147456]{1,0:T(8,128)(2,1)} dynamic-update-slice(bf16[8,147456]{1,0:T(8,128)(2,1)} %get-tuple-element.234, bf16[1,147456]{1,0:T(2,128)(2,1)S(1)} %convert_element_type.104, s32[]{:T(128)} %get-tuple-element.233, s32[]{:T(128)} %constant.88.clone.1..sunk) | dynamic-update-slice | bytes 589828 | tf_op jit(solution)/shard_map/while/body/jit(dynamic_update_index_in_dim)/dynamic_update_slice | solution.py:69
  28.5 2.6 reshape.309
  31.0 1.9 convolution_bitcast_fusion.2
  33.0 1.9 fusion.48
  34.9 4.6 copy.33
  41.6 11.5 %dynamic_update_slice.13 = bf16[8,147456]{1,0:T(8,128)(2,1)} dynamic-update-slice(bf16[8,147456]{1,0:T(8,128)(2,1)} %get-tuple-element.234, bf16[1,147456]{1,0:T(2,128)(2,1)S(1)} %convert_element_type.104, s32[]{:T(128)} %get-tuple-element.233, s32[]{:T(128)} %constant.88.clone.1..sunk) | dynamic-update-slice | bytes 589828 | tf_op jit(solution)/shard_map/while/body/jit(dynamic_update_index_in_dim)/dynamic_update_slice | solution.py:69
  54.4 2.6 reshape.309
  57.0 1.9 convolution_bitcast_fusion.2
  59.0 1.9 fusion.48
  60.9 4.6 copy.33
  67.6 11.5 %dynamic_update_slice.13 = bf16[8,147456]{1,0:T(8,128)(2,1)} dynamic-update-slice(bf16[8,147456]{1,0:T(8,128)(2,1)} %get-tuple-element.234, bf16[1,147456]{1,0:T(2,128)(2,1)S(1)} %convert_element_type.104, s32[]{:T(128)} %get-tuple-element.233, s32[]{:T(128)} %constant.88.clone.1..sunk) | dynamic-update-slice | bytes 589828 | tf_op jit(solution)/shard_map/while/body/jit(dynamic_update_index_in_dim)/dynamic_update_slice | solution.py:69
  80.4 2.6 reshape.309
  83.0 1.9 convolution_bitcast_fusion.2
  84.9 1.9 fusion.48
  86.9 4.6 copy.33
  93.6 11.5 %dynamic_update_slice.13 = bf16[8,147456]{1,0:T(8,128)(2,1)} dynamic-update-slice(bf16[8,147456]{1,0:T(8,128)(2,1)} %get-tuple-element.234, bf16[1,147456]{1,0:T(2,128)(2,1)S(1)} %convert_element_type.104, s32[]{:T(128)} %get-tuple-element.233, s32[]{:T(128)} %constant.88.clone.1..sunk) | dynamic-update-slice | bytes 589828 | tf_op jit(solution)/shard_map/while/body/jit(dynamic_update_index_in_dim)/dynamic_update_slice | solution.py:69
  106.4 2.6 reshape.309
  109.0 1.9 convolution_bitcast_fusion.2
  110.9 1.9 fusion.48
  112.9 4.6 copy.33
  119.6 11.5 %dynamic_update_slice.13 = bf16[8,147456]{1,0:T(8,128)(2,1)} dynamic-update-slice(bf16[8,147456]{1,0:T(8,128)(2,1)} %get-tuple-element.234, bf16[1,147456]{1,0:T(2,128)(2,1)S(1)} %convert_element_type.104, s32[]{:T(128)} %get-tuple-element.233, s32[]{:T(128)} %constant.88.clone.1..sunk) | dynamic-update-slice | bytes 589828 | tf_op jit(solution)/shard_map/while/body/jit(dynamic_update_index_in_dim)/dynamic_update_slice | solution.py:69
  132.4 2.6 reshape.309
  135.0 1.9 convolution_bitcast_fusion.2
  136.9 1.9 fusion.48
  138.9 4.6 copy.33
  145.6 11.5 %dynamic_update_slice.13 = bf16[8,147456]{1,0:T(8,128)(2,1)} dynamic-update-slice(bf16[8,147456]{1,0:T(8,128)(2,1)} %get-tuple-element.234, bf16[1,147456]{1,0:T(2,128)(2,1)S(1)} %convert_element_type.104, s32[]{:T(128)} %get-tuple-element.233, s32[]{:T(128)} %constant.88.clone.1..sunk) | dynamic-update-slice | bytes 589828 | tf_op jit(solution)/shard_map/while/body/jit(dynamic_update_index_in_dim)/dynamic_update_slice | solution.py:69
  158.4 2.6 reshape.309
  162.9 1.9 fusion.48
  164.8 4.6 copy.33
  171.6 11.5 %dynamic_update_slice.13 = bf16[8,147456]{1,0:T(8,128)(2,1)} dynamic-update-slice(bf16[8,147456]{1,0:T(8,128)(2,1)} %get-tuple-element.234, bf16[1,147456]{1,0:T(2,128)(2,1)S(1)} %convert_element_type.104, s32[]{:T(128)} %get-tuple-element.233, s32[]{:T(128)} %constant.88.clone.1..sunk) | dynamic-update-slice | bytes 589828 | tf_op jit(solution)/shard_map/while/body/jit(dynamic_update_index_in_dim)/dynamic_update_slice | solution.py:69
  184.4 2.6 reshape.309
  187.0 1.9 convolution_bitcast_fusion.2
  188.9 1.9 fusion.48
  190.8 4.6 copy.33
  197.6 11.5 %dynamic_update_slice.13 = bf16[8,147456]{1,0:T(8,128)(2,1)} dynamic-update-slice(bf16[8,147456]{1,0:T(8,128)(2,1)} %get-tuple-element.234, bf16[1,147456]{1,0:T(2,128)(2,1)S(1)} %convert_element_type.104, s32[]{:T(128)} %get-tuple-element.233, s32[]{:T(128)} %constant.88.clone.1..sunk) | dynamic-update-slice | bytes 589828 | tf_op jit(solution)/shard_map/while/body/jit(dynamic_update_index_in_dim)/dynamic_update_slice | solution.py:69
  209.1 7.5 %all-to-all-start = ((bf16[8,16,9216]{2,0,1:T(8,128)(2,1)}), bf16[8,16,9216]{2,0,1:T(8,128)(2,1)S(1)}, u32[]{:S(2)}, u32[]{:S(2)}) async-start(bf16[8,16,9216]{2,0,1:T(8,128)(2,1)} %bitcast.70), calls=%async_computation | async-start | bytes 4718592 | tf_op jit(solution)/shard_map/all_to_all | solution.py:79
  216.6 54.9 %all-gather = s32[16,8,3]{1,2,0:T(4,128)S(1)} all-gather(s32[1,8,3]{1,2,0:T(4,128)S(1)} %bitcast.76), channel_id=1, replica_groups=mesh['groups'=2,'tm'=16] {'tm'}, dimensions={0}, use_global_device_ids=true | all-gather | bytes 1632 | tf_op jit(solution)/shard_map/all_gather | solution.py:70
  271.7 2.9 fusion.18
  274.7 12.8 %all-to-all-start.1 = ((f32[16,8,9216]{2,1,0:T(8,128)}), f32[16,8,9216]{2,1,0:T(8,128)}, u32[]{:S(2)}, u32[]{:S(2)}) async-start(f32[16,8,9216]{2,1,0:T(8,128)} %fusion.18), calls=%async_computation.1 | async-start | bytes 9437184 | tf_op jit(solution)/shard_map/all_to_all | solution.py:82
  287.5 86.7 %all-to-all-done.1 = f32[16,8,9216]{2,1,0:T(8,128)} async-done(((f32[16,8,9216]{2,1,0:T(8,128)}), f32[16,8,9216]{2,1,0:T(8,128)}, u32[]{:S(2)}, u32[]{:S(2)}) %all-to-all-start.1) | async-done | bytes 4718624 | tf_op jit(solution)/shard_map/all_to_all | solution.py:82
  374.3 265.4 %while.24 = (s32[]{:T(128)}, f32[8,2048]{1,0:T(8,128)}, f32[8,147456]{1,0:T(8,128)}, f32[2048,48]{0,1:T(8,128)S(1)}, f32[48,2048]{1,0:T(8,128)S(1)}, /*index=5*/s32[]{:T(128)}, s32[]{:T(128)}) while((s32[]{:T(128)}, f32[8,2048]{1,0:T(8,128)}, f32[8,147456]{1,0:T(8,128)}, f32[2048,48]{0,1:T(8,128)S(1)}, f32[48,2048]{1,0:T(8,128)S(1)}, ...), condition=%wide.region_9.10_spmd.clone, body=%wide.region_3.9_spmd.clone.sunk | while | flops 3643499264 | bytes 4941397 | solution.py:97
  374.3 7.7 %dynamic-slice_reduce_fusion.2 = f32[147456]{0:T(1024)S(1)} fusion(f32[8,147456]{1,0:T(8,128)} %get-tuple-element.261, s32[]{:T(128)} %get-tuple-element.252), kind=kLoop, calls=%fused_computation.14.clone.1 | loop fusion | bytes 1179652 | tf_op jit(solution)/shard_map/while/body/jit(dynamic_index_in_dim)/dynamic_slice | solution.py:97
  382.6 22.8 %multiply_reduce_fusion.7 = (f32[2048]{0:T(1024)S(1)}, f32[64,2048]{1,0:T(8,128)S(1)}) fusion(f32[48,2048]{1,0:T(8,128)S(1)} %get-tuple-element.263, f32[64,48,48]{2,1,0:T(8,128)S(1)} %dot_general.20, f32[2048,48]{0,1:T(8,128)S(1)} %get-tuple-element.262), kind=kOutput, calls=%fused_computation.12.clone.1 | convolution fusion | flops 3642619904 | bytes 1908736 | tf_op jit(solution)/shard_map/while/body/eval_jaxpr/dot_general | solution.py:85
  407.4 7.7 %dynamic-slice_reduce_fusion.2 = f32[147456]{0:T(1024)S(1)} fusion(f32[8,147456]{1,0:T(8,128)} %get-tuple-element.261, s32[]{:T(128)} %get-tuple-element.252), kind=kLoop, calls=%fused_computation.14.clone.1 | loop fusion | bytes 1179652 | tf_op jit(solution)/shard_map/while/body/jit(dynamic_index_in_dim)/dynamic_slice | solution.py:97
  415.8 22.8 %multiply_reduce_fusion.7 = (f32[2048]{0:T(1024)S(1)}, f32[64,2048]{1,0:T(8,128)S(1)}) fusion(f32[48,2048]{1,0:T(8,128)S(1)} %get-tuple-element.263, f32[64,48,48]{2,1,0:T(8,128)S(1)} %dot_general.20, f32[2048,48]{0,1:T(8,128)S(1)} %get-tuple-element.262), kind=kOutput, calls=%fused_computation.12.clone.1 | convolution fusion | flops 3642619904 | bytes 1908736 | tf_op jit(solution)/shard_map/while/body/eval_jaxpr/dot_general | solution.py:85
  440.6 7.7 %dynamic-slice_reduce_fusion.2 = f32[147456]{0:T(1024)S(1)} fusion(f32[8,147456]{1,0:T(8,128)} %get-tuple-element.261, s32[]{:T(128)} %get-tuple-element.252), kind=kLoop, calls=%fused_computation.14.clone.1 | loop fusion | bytes 1179652 | tf_op jit(solution)/shard_map/while/body/jit(dynamic_index_in_dim)/dynamic_slice | solution.py:97
  449.0 22.8 %multiply_reduce_fusion.7 = (f32[2048]{0:T(1024)S(1)}, f32[64,2048]{1,0:T(8,128)S(1)}) fusion(f32[48,2048]{1,0:T(8,128)S(1)} %get-tuple-element.263, f32[64,48,48]{2,1,0:T(8,128)S(1)} %dot_general.20, f32[2048,48]{0,1:T(8,128)S(1)} %get-tuple-element.262), kind=kOutput, calls=%fused_computation.12.clone.1 | convolution fusion | flops 3642619904 | bytes 1908736 | tf_op jit(solution)/shard_map/while/body/eval_jaxpr/dot_general | solution.py:85
  473.8 7.7 %dynamic-slice_reduce_fusion.2 = f32[147456]{0:T(1024)S(1)} fusion(f32[8,147456]{1,0:T(8,128)} %get-tuple-element.261, s32[]{:T(128)} %get-tuple-element.252), kind=kLoop, calls=%fused_computation.14.clone.1 | loop fusion | bytes 1179652 | tf_op jit(solution)/shard_map/while/body/jit(dynamic_index_in_dim)/dynamic_slice | solution.py:97
  482.1 22.8 %multiply_reduce_fusion.7 = (f32[2048]{0:T(1024)S(1)}, f32[64,2048]{1,0:T(8,128)S(1)}) fusion(f32[48,2048]{1,0:T(8,128)S(1)} %get-tuple-element.263, f32[64,48,48]{2,1,0:T(8,128)S(1)} %dot_general.20, f32[2048,48]{0,1:T(8,128)S(1)} %get-tuple-element.262), kind=kOutput, calls=%fused_computation.12.clone.1 | convolution fusion | flops 3642619904 | bytes 1908736 | tf_op jit(solution)/shard_map/while/body/eval_jaxpr/dot_general | solution.py:85
  507.0 7.7 %dynamic-slice_reduce_fusion.2 = f32[147456]{0:T(1024)S(1)} fusion(f32[8,147456]{1,0:T(8,128)} %get-tuple-element.261, s32[]{:T(128)} %get-tuple-element.252), kind=kLoop, calls=%fused_computation.14.clone.1 | loop fusion | bytes 1179652 | tf_op jit(solution)/shard_map/while/body/jit(dynamic_index_in_dim)/dynamic_slice | solution.py:97
  515.3 22.8 %multiply_reduce_fusion.7 = (f32[2048]{0:T(1024)S(1)}, f32[64,2048]{1,0:T(8,128)S(1)}) fusion(f32[48,2048]{1,0:T(8,128)S(1)} %get-tuple-element.263, f32[64,48,48]{2,1,0:T(8,128)S(1)} %dot_general.20, f32[2048,48]{0,1:T(8,128)S(1)} %get-tuple-element.262), kind=kOutput, calls=%fused_computation.12.clone.1 | convolution fusion | flops 3642619904 | bytes 1908736 | tf_op jit(solution)/shard_map/while/body/eval_jaxpr/dot_general | solution.py:85
  540.2 7.7 %dynamic-slice_reduce_fusion.2 = f32[147456]{0:T(1024)S(1)} fusion(f32[8,147456]{1,0:T(8,128)} %get-tuple-element.261, s32[]{:T(128)} %get-tuple-element.252), kind=kLoop, calls=%fused_computation.14.clone.1 | loop fusion | bytes 1179652 | tf_op jit(solution)/shard_map/while/body/jit(dynamic_index_in_dim)/dynamic_slice | solution.py:97
  548.5 22.8 %multiply_reduce_fusion.7 = (f32[2048]{0:T(1024)S(1)}, f32[64,2048]{1,0:T(8,128)S(1)}) fusion(f32[48,2048]{1,0:T(8,128)S(1)} %get-tuple-element.263, f32[64,48,48]{2,1,0:T(8,128)S(1)} %dot_general.20, f32[2048,48]{0,1:T(8,128)S(1)} %get-tuple-element.262), kind=kOutput, calls=%fused_computation.12.clone.1 | convolution fusion | flops 3642619904 | bytes 1908736 | tf_op jit(solution)/shard_map/while/body/eval_jaxpr/dot_general | solution.py:85
  573.3 7.7 %dynamic-slice_reduce_fusion.2 = f32[147456]{0:T(1024)S(1)} fusion(f32[8,147456]{1,0:T(8,128)} %get-tuple-element.261, s32[]{:T(128)} %get-tuple-element.252), kind=kLoop, calls=%fused_computation.14.clone.1 | loop fusion | bytes 1179652 | tf_op jit(solution)/shard_map/while/body/jit(dynamic_index_in_dim)/dynamic_slice | solution.py:97
  581.7 22.8 %multiply_reduce_fusion.7 = (f32[2048]{0:T(1024)S(1)}, f32[64,2048]{1,0:T(8,128)S(1)}) fusion(f32[48,2048]{1,0:T(8,128)S(1)} %get-tuple-element.263, f32[64,48,48]{2,1,0:T(8,128)S(1)} %dot_general.20, f32[2048,48]{0,1:T(8,128)S(1)} %get-tuple-element.262), kind=kOutput, calls=%fused_computation.12.clone.1 | convolution fusion | flops 3642619904 | bytes 1908736 | tf_op jit(solution)/shard_map/while/body/eval_jaxpr/dot_general | solution.py:85
  606.5 7.7 %dynamic-slice_reduce_fusion.2 = f32[147456]{0:T(1024)S(1)} fusion(f32[8,147456]{1,0:T(8,128)} %get-tuple-element.261, s32[]{:T(128)} %get-tuple-element.252), kind=kLoop, calls=%fused_computation.14.clone.1 | loop fusion | bytes 1179652 | tf_op jit(solution)/shard_map/while/body/jit(dynamic_index_in_dim)/dynamic_slice | solution.py:97
  614.9 22.8 %multiply_reduce_fusion.7 = (f32[2048]{0:T(1024)S(1)}, f32[64,2048]{1,0:T(8,128)S(1)}) fusion(f32[48,2048]{1,0:T(8,128)S(1)} %get-tuple-element.263, f32[64,48,48]{2,1,0:T(8,128)S(1)} %dot_general.20, f32[2048,48]{0,1:T(8,128)S(1)} %get-tuple-element.262), kind=kOutput, calls=%fused_computation.12.clone.1 | convolution fusion | flops 3642619904 | bytes 1908736 | tf_op jit(solution)/shard_map/while/body/eval_jaxpr/dot_general | solution.py:85
  639.7 22.4 %all-to-all-start.2 = ((f32[8,16,128]{2,0,1:T(8,128)}), f32[8,16,128]{2,0,1:T(8,128)S(1)}, u32[]{:S(2)}, u32[]{:S(2)}) async-start(f32[8,16,128]{2,0,1:T(8,128)} %bitcast.11), calls=%async_computation.2 | async-start | bytes 131072 | tf_op jit(solution)/shard_map/all_to_all | solution.py:98
  662.2 6.8 %all-to-all-done.2 = f32[8,16,128]{2,0,1:T(8,128)S(1)} async-done(((f32[8,16,128]{2,0,1:T(8,128)}), f32[8,16,128]{2,0,1:T(8,128)S(1)}, u32[]{:S(2)}, u32[]{:S(2)}) %all-to-all-start.2) | async-done | bytes 65568 | tf_op jit(solution)/shard_map/all_to_all | solution.py:98
  (135 shorter events, 52.4 us)
Async XLA Ops:
  209.1 7.5 %copy-start.1 = (s32[8,3]{0,1:T(4,128)S(1)}, s32[8,3]{0,1:T(4,128)}, u32[]{:S(2)}) copy-start(s32[8,3]{0,1:T(4,128)} %param.8) | copy-start | bytes 292
  209.1 62.7 %all-to-all-start = ((bf16[8,16,9216]{2,0,1:T(8,128)(2,1)}), bf16[8,16,9216]{2,0,1:T(8,128)(2,1)S(1)}, u32[]{:S(2)}, u32[]{:S(2)}) async-start(bf16[8,16,9216]{2,0,1:T(8,128)(2,1)} %bitcast.70), calls=%async_computation | async-start | bytes 4718592 | tf_op jit(solution)/shard_map/all_to_all | solution.py:79
  274.7 12.8 %copy-start = (bf16[2048,48]{0,1:T(8,128)(2,1)S(1)}, bf16[2048,48]{0,1:T(8,128)(2,1)}, u32[]{:S(2)}) copy-start(bf16[2048,48]{0,1:T(8,128)(2,1)} %param.9) | copy-start | bytes 589828
  274.7 99.6 %all-to-all-start.1 = ((f32[16,8,9216]{2,1,0:T(8,128)}), f32[16,8,9216]{2,1,0:T(8,128)}, u32[]{:S(2)}, u32[]{:S(2)}) async-start(f32[16,8,9216]{2,1,0:T(8,128)} %fusion.18), calls=%async_computation.1 | async-start | bytes 9437184 | tf_op jit(solution)/shard_map/all_to_all | solution.py:82
  639.7 29.3 %all-to-all-start.2 = ((f32[8,16,128]{2,0,1:T(8,128)}), f32[8,16,128]{2,0,1:T(8,128)S(1)}, u32[]{:S(2)}, u32[]{:S(2)}) async-start(f32[8,16,128]{2,0,1:T(8,128)} %bitcast.11), calls=%async_computation.2 | async-start | bytes 131072 | tf_op jit(solution)/shard_map/all_to_all | solution.py:98
where the time goes:
time: 674 us; the launch traced here: 670 us
  local copies, waits for them, and re-layouts  247 us (37%)
  matrix products  208 us (31%)
  waiting for transfers between devices  93.5 us (14%)
  blocking collectives  54.9 us (8%)
  starting transfers between devices  42.7 us (6%)
  other arithmetic  22 us (3%)
    dot_general x8, matrix products, bin_damage(): lax.dot_general(flat_mean.reshape(freq_count * channels, channels), weigh...  182 us
    dynamic_update_slice x8, local copies, waits for them, and re-layouts, per_device(): lax.map(lambda one_block: block_spectra(one_block, dft_table), strain)  91.7 us
    all_to_all x1, waiting for transfers between devices, per_device(): lax.all_to_all(mean_cospec, 'tm', split_axis=0, concat_axis=1, tiled=True)  86.7 us
    dynamic_slice x8, local copies, waits for them, and re-layouts, per_device(): owned_damage = lax.map(bin_damage, owned_bins)  61.9 us
    all_gather x1, blocking collectives, per_device(): all_labels = lax.all_gather(bin_labels, 'tm', axis=0, tiled=True)  54.9 us
    convert_element_type x8, local copies, waits for them, and re-layouts, block_spectra(): (product[:SEGLEN, :, :-1] + product[SEGLEN:, :, 1:]).astype(jnp.bfloat16)  36.5 us
    all_to_all x1, starting transfers between devices, per_device(): lax.all_to_all(owned_damage, 'tm', split_axis=1, concat_axis=0, tiled=True)  22.4 us
    reshape x8, local copies, waits for them, and re-layouts, block_spectra(): pieces = one_block.reshape(channels, NSEG + 1, half_len)  20.6 us
  transfers between devices with their start and end apart: 3, of which 2 were waited for; matrix products, arithmetic and copies ran while one was open for 0% of the time, Pallas kernels for 0%

commit v1 on v0

v1 whole, which is shorter than its diff:
```python
import functools
import math

import jax
import jax.numpy as jnp
from jax import lax
from jax.experimental import pallas as pl
from jax.experimental.pallas import tpu as pltpu
from jax.sharding import PartitionSpec as P

SEGLEN = 128
NSEG = 187
NDIR = 8
NYAW = 2
NBIN = 128
LANES = 128
HALF = SEGLEN // 2
CPAD = 64
NMOM = 4
NT = (((1,), (1,)), ((), ()))


def build_table():
    positions = jnp.arange(SEGLEN, dtype=jnp.int32)
    harmonic = jnp.arange(1, SEGLEN // 2 + 1, dtype=jnp.int32)
    phase = (positions[:, None] * harmonic[None, :] % SEGLEN).astype(jnp.float32) * (
        2.0 * math.pi / SEGLEN
    )
    window = 0.5 - 0.5 * jnp.cos(positions.astype(jnp.float32) * (2.0 * math.pi / SEGLEN))
    return jnp.concatenate(
        [window[:, None] * jnp.cos(phase), window[:, None] * jnp.sin(phase)], axis=1
    ).astype(jnp.bfloat16)


def pair_table():
    columns = build_table().T
    even = jnp.pad(columns, ((0, 0), (0, SEGLEN)))
    odd = jnp.pad(columns, ((0, 0), (HALF, HALF)))
    return jnp.concatenate([even, odd], axis=0)


def split3(value):
    high = value.astype(jnp.bfloat16)
    rest = value - high.astype(jnp.float32)
    middle = rest.astype(jnp.bfloat16)
    low = (rest - middle.astype(jnp.float32)).astype(jnp.bfloat16)
    return high, middle, low


def moments_kernel(
    blocks, channels, tiles, labels, strain, table, influence, out, xs, even, odd, weights, columns, parts
):
    block = pl.program_id(0)
    hotspots = influence.shape[0]
    freq_count = SEGLEN // 2
    rows = xs.shape[0] // channels

    @pl.when(block == 0)
    def _():
        xs[...] = jnp.zeros_like(xs)
        even[...] = jnp.zeros_like(even)
        odd[...] = jnp.zeros_like(odd)
        weights[...] = jnp.zeros_like(weights)
        for part in range(3):
            weights[:, part * CPAD : part * CPAD + channels] = influence[...]
        row = lax.broadcasted_iota(jnp.int32, (channels, channels), 0)
        col = lax.broadcasted_iota(jnp.int32, (channels, channels), 1)
        eye = jnp.where(row == col, 1.0, 0.0).astype(jnp.bfloat16)
        columns[...] = lax.dot_general(eye, influence[...], NT, preferred_element_type=jnp.float32)

    for tile in range(tiles):
        xs[tile * channels : (tile + 1) * channels, :] = strain[
            0, :, tile * LANES : (tile + 1) * LANES
        ].astype(jnp.float32)

    pair_rows = table[...]

    def transform(pair, carry):
        windows = []
        for offset in range(2):
            channel = 2 * pair + offset
            here = xs[pl.ds(channel, LANES, stride=channels), :].astype(jnp.bfloat16)
            after = xs[pl.ds(channel + channels, LANES, stride=channels), :].astype(jnp.bfloat16)
            windows.append(jnp.concatenate([here, after], axis=1))
        window = jnp.concatenate(windows, axis=0)
        coeffs = lax.dot_general(pair_rows, window, NT, preferred_element_type=jnp.float32)
        for offset in range(2):
            channel = 2 * pair + offset
            lanes = slice(offset * LANES, (offset + 1) * LANES)
            even[pl.ds(channel, SEGLEN, stride=CPAD), :] = coeffs[:SEGLEN, lanes]
            odd[pl.ds(channel, SEGLEN, stride=CPAD), :] = coeffs[SEGLEN:, lanes]
        return carry

    lax.fori_loop(0, channels // 2, transform, 0, unroll=2)

    lane = lax.broadcasted_iota(jnp.int32, (1, LANES), 1)
    keep_odd = lane < tiles - 1
    first_half = lane < CPAD
    scale = 8.0 / (3.0 * SEGLEN * NSEG)

    def cross(pair, totals):
        pieces = []
        for base in (0, freq_count):
            start = pl.multiple_of((base + 2 * pair) * CPAD, 2 * CPAD)
            pieces.append(even[pl.ds(start, 2 * CPAD), :].astype(jnp.bfloat16))
            pieces.append(
                jnp.where(keep_odd, odd[pl.ds(start, 2 * CPAD), :], 0.0).astype(jnp.bfloat16)
            )
        right = jnp.concatenate(pieces, axis=1)
        left = jnp.concatenate([right[:channels], right[CPAD : CPAD + channels]], axis=0)
        product = lax.dot_general(left, right, NT, preferred_element_type=jnp.float32)
        cospec = jnp.where(first_half, product[:channels], product[channels:]) * scale
        cospec = cospec.astype(jnp.bfloat16).astype(jnp.float32)
        index = 2 * pair + 1 + jnp.where(first_half, 0, 1)
        frequency = index.astype(jnp.float32) / SEGLEN
        square = frequency * frequency
        return (
            totals[0] + cospec,
            totals[1] + cospec * frequency,
            totals[2] + cospec * square,
            totals[3] + cospec * (square * square),
        )

    zero = jnp.zeros((channels, LANES), jnp.float32)
    totals = lax.fori_loop(0, freq_count // 2, cross, (zero,) * NMOM, unroll=2)
    for moment in range(NMOM):
        whole = totals[moment] + pltpu.roll(totals[moment], CPAD, 1)
        high, middle, low = split3(whole * (1.0 / SEGLEN))
        start = pl.multiple_of((moment * blocks + block) * channels, 16)
        parts[pl.ds(start, channels), :LANES] = jnp.where(first_half, high, middle)
        parts[pl.ds(start, channels), LANES:] = low

    @pl.when(block == blocks - 1)
    def _():
        width = 2 * LANES

        def project(step, carry):
            start = pl.multiple_of(step * width, width)
            spread = lax.dot_general(
                parts[...], weights[pl.ds(start, width), :], NT, preferred_element_type=jnp.float32
            )
            spread = spread.reshape(NMOM * blocks, channels, width)
            moments = jnp.sum(spread * columns[:, pl.ds(start, width)][None], axis=1)
            for half in range(2):
                for moment in range(NMOM):
                    out[2 * step + half, moment] = moments[
                        moment * blocks : (moment + 1) * blocks, half * LANES : (half + 1) * LANES
                    ]
            return carry

        lax.fori_loop(0, hotspots // width, project, 0)
        row = lax.broadcasted_iota(jnp.int32, (blocks, LANES), 0)
        named = jnp.zeros((blocks, LANES), jnp.float32)
        for index in range(blocks):
            label = (labels[index, 0] * NDIR + labels[index, 1]) * NYAW + labels[index, 2]
            named = jnp.where(row == index, label.astype(jnp.float32), named)
        for step in range(hotspots // LANES):
            out[step, NMOM] = named


def local_moments(strain, bin_labels, influence):
    blocks, channels, samples = strain.shape
    hotspots = influence.shape[0]
    tiles = samples // LANES
    table = pair_table()
    return pl.pallas_call(
        functools.partial(moments_kernel, blocks, channels, tiles),
        grid=(blocks,),
        in_specs=[
            pl.BlockSpec(memory_space=pltpu.SMEM),
            pl.BlockSpec((1, channels, samples), lambda b: (b, 0, 0)),
            pl.BlockSpec((2 * SEGLEN, 2 * SEGLEN), lambda b: (0, 0)),
            pl.BlockSpec((hotspots, channels), lambda b: (0, 0)),
        ],
        out_specs=pl.BlockSpec((hotspots // LANES, NMOM + 1, blocks, LANES), lambda b: (0, 0, 0, 0)),
        out_shape=jax.ShapeDtypeStruct((hotspots // LANES, NMOM + 1, blocks, LANES), jnp.float32),
        scratch_shapes=[
            pltpu.VMEM(((LANES + 1) * channels, LANES), jnp.float32),
            pltpu.VMEM((SEGLEN * CPAD, LANES), jnp.float32),
            pltpu.VMEM((SEGLEN * CPAD, LANES), jnp.float32),
            pltpu.VMEM((hotspots, 2 * LANES), jnp.bfloat16),
            pltpu.VMEM((channels, hotspots), jnp.float32),
            pltpu.VMEM((NMOM * blocks * channels, 2 * LANES), jnp.bfloat16),
        ],
        compiler_params=pltpu.CompilerParams(vmem_limit_bytes=48 << 20),
        name="block_moments",
    )(bin_labels, strain, table, influence)


def dirlik(moment_zero, moment_one, moment_two, moment_four):
    spread_ratio = moment_two / jnp.sqrt(moment_zero * moment_four)
    mean_freq = moment_one / moment_zero * jnp.sqrt(moment_two / moment_four)
    d_one = 2.0 * (mean_freq - spread_ratio**2) / (1.0 + spread_ratio**2)
    shared = 1.0 - spread_ratio - d_one + d_one**2
    r_ratio = (spread_ratio - mean_freq - d_one**2) / shared
    d_two = shared / (1.0 - r_ratio)
    d_three = 1.0 - d_one - d_two
    q_factor = 1.25 * (spread_ratio - d_three - d_two * r_ratio) / d_one
    peak_rate = jnp.sqrt(moment_four / moment_two)
    bracket = 6.0 * d_one * q_factor**3 + 2.8284271247 * 1.3293403882 * (
        jnp.abs(r_ratio) ** 3 * d_two + d_three
    )
    return peak_rate * (2.0 * jnp.sqrt(moment_zero)) ** 3 * bracket


def damage_kernel(received, damage, total):
    sources, _, blocks, width = received.shape
    count_blocks = sources * blocks
    named = received[:, NMOM].reshape(count_blocks, width)[:, :1]
    bins = lax.broadcasted_iota(jnp.int32, (count_blocks, NBIN), 1).astype(jnp.float32)
    member = jnp.where(named == bins, 1.0, 0.0)
    chosen = member.T.astype(jnp.bfloat16)
    count = jnp.sum(member.T, axis=1, keepdims=True)
    means = []
    for moment in range(NMOM):
        total_moment = jnp.zeros((NBIN, width), jnp.float32)
        for piece in split3(received[:, moment].reshape(count_blocks, width)):
            total_moment = total_moment + jnp.dot(chosen, piece, preferred_element_type=jnp.float32)
        means.append(total_moment / count)
    by_bin = dirlik(*means)
    damage[...] = by_bin
    total[...] = jnp.sum(count / count_blocks * by_bin, axis=0, keepdims=True)


def per_device(strain, bin_labels, influence):
    devices = lax.axis_size("tm")
    blocks = strain.shape[0]
    hotspots = influence.shape[0]
    width = hotspots // devices
    moments = local_moments(strain, bin_labels, influence)
    if width != LANES:
        share = LANES // width
        moments = moments.reshape(hotspots // LANES, NMOM + 1, blocks, share, width)
        moments = moments.transpose(0, 3, 1, 2, 4).reshape(devices, NMOM + 1, blocks, width)
    received = lax.all_to_all(moments, "tm", split_axis=0, concat_axis=0, tiled=True)
    damage, total = pl.pallas_call(
        damage_kernel,
        out_shape=(
            jax.ShapeDtypeStruct((NBIN, width), jnp.float32),
            jax.ShapeDtypeStruct((1, width), jnp.float32),
        ),
        name="bin_damage",
    )(received)
    return damage, total.reshape(width)


def solution(mesh):
    placed = (P(("groups", "tm"), None, None), P(("groups", "tm"), None), P())
    return jax.shard_map(
        per_device,
        mesh=mesh,
        in_specs=placed,
        out_specs=(P("groups", "tm"), P(("groups", "tm"))),
        check_vma=False,
    )
```

time: 674 us -> 119 us (0.18)
  local copies, waits for them, and re-layouts: 247 us -> 1.96 us
  matrix products: 208 us -> 0 us
  Pallas kernels: 0 us -> 97.5 us
  waiting for transfers between devices: 93.5 us -> 0 us
  starting transfers between devices: 42.7 us -> 0 us
  blocking collectives: 54.9 us -> 18.4 us
  other arithmetic: 22 us -> 0.35 us
    dot_general x25 -> x0, matrix products: 208 us -> none  [the longest x8 182 us: bin_damage(): lax.dot_general(flat_mean.reshape(freq_count * channels, channels), weigh...]
    dynamic_update_slice x16 -> x0, local copies, waits for them, and re-layouts: 104 us -> none  [the longest x8 91.7 us: per_device(): lax.map(lambda one_block: block_spectra(one_block, dft_table), strain)]
    pallas_call x0 -> x2, Pallas kernels: none -> 97.5 us  [the longest x1 95.3 us: local_moments(): pl.pallas_call(functools.partial(moments_kernel, blocks, channels, tiles)...]
    all_to_all x3 -> x0, waiting for transfers between devices: 93.5 us -> none  [the longest x1 86.7 us: per_device(): lax.all_to_all(mean_cospec, 'tm', split_axis=0, concat_axis=1, tiled=True)]
    dynamic_slice x16 -> x0, local copies, waits for them, and re-layouts: 72.6 us -> none  [the longest x8 61.9 us: per_device(): owned_damage = lax.map(bin_damage, owned_bins)]
    all_gather x1 -> x0, blocking collectives: 54.9 us -> none  [per_device(): all_labels = lax.all_gather(bin_labels, 'tm', axis=0, tiled=True)]
    convert_element_type x16 -> x0, local copies, waits for them, and re-layouts: 44.5 us -> none  [the longest x8 36.5 us: block_spectra(): (product[:SEGLEN, :, :-1] + product[SEGLEN:, :, 1:]).astype(jnp.bfloat16)]
    all_to_all x3 -> x0, starting transfers between devices: 42.7 us -> none  [the longest x1 22.4 us: per_device(): lax.all_to_all(owned_damage, 'tm', split_axis=1, concat_axis=0, tiled=True)]
  transfers between devices with their start and end apart: 3 -> 0, of which waited for: 2 -> 0; matrix products, arithmetic and copies ran while one was open for 0% -> 0% of each run, Pallas kernels for 0% -> 0%
where the time goes in v1:
time: 119 us
  Pallas kernels  97.5 us (82%)
  blocking collectives  18.4 us (15%)
  local copies, waits for them, and re-layouts  1.96 us (2%)
    pallas_call x1, Pallas kernels, local_moments(): pl.pallas_call(functools.partial(moments_kernel, blocks, channels, tiles)...  95.3 us
    all_to_all x1, blocking collectives, per_device(): lax.all_to_all(moments, 'tm', split_axis=0, concat_axis=0, tiled=True)  18.4 us

profile of v1, /device:TPU:0, one launch (start us, length us, event | category | flops | bytes accessed | tf_op | source)
XLA Modules:
  0.0 118.9 jit_solution(17860641008152689957)
XLA Ops:
  0.7 0.8 copy.5.labels
  1.4 0.2 multiply_convert_fusion.1
  1.7 0.1 fusion.2.table
  1.8 1.2 %copy.6.influence = bf16[2048,48]{1,0:T(8,128)(2,1)S(1)} copy(bf16[2048,48]{0,1:T(8,128)(2,1)} %param.5) | data formatting | bytes 393216 | tf_op args[2]
  3.0 95.3 %block_moments.1 = f32[16,5,8,128]{3,2,1,0:T(8,128)S(1)} custom-call(s32[8,3]{1,0:T(8,128)S(1)} %copy.5.labels, bf16[8,48,12032]{2,1,0:T(8,128)(2,1)} %strain.1, bf16[256,256]{1,0:T(8,128)(2,1)S(1)} %fusion.2.table, bf16[2048,48]{1,0:T(8,128)(2,1)S(1)} %copy.6.influence), custom_call_target="tpu_custom_call" | custom-call | tf_op jit(solution)/shard_map/block_moments/pallas_call | solution.py:166
  98.3 18.4 %all_to_all.5.received = f32[16,5,8,128]{3,2,1,0:T(8,128)} all-to-all(f32[16,5,8,128]{3,2,1,0:T(8,128)S(1)} %block_moments.1), channel_id=1, replica_groups=mesh['groups'=2,'tm'=16] {'tm'}, dimensions={0} | all-to-all | bytes 655360 | tf_op jit(solution)/shard_map/all_to_all | solution.py:235
  116.7 2.2 %bin_damage.1 = (f32[128,128]{1,0:T(8,128)}, f32[1,128]{1,0:T(1,128)}) custom-call(f32[16,5,8,128]{3,2,1,0:T(8,128)} %all_to_all.5.received), custom_call_target="tpu_custom_call" | custom-call | tf_op jit(solution)/shard_map/bin_damage/pallas_call | solution.py:236
  (3 shorter events, 0.1 us)

commit v2 on v1

v2 whole, which is shorter than its diff:
```python
import functools
import math

import jax
import jax.numpy as jnp
import ml_dtypes
import numpy as np
from jax import lax
from jax.experimental import pallas as pl
from jax.experimental.pallas import tpu as pltpu
from jax.sharding import PartitionSpec as P

SEGLEN = 128
NSEG = 187
NDIR = 8
NYAW = 2
NBIN = 128
LANES = 128
HALF = SEGLEN // 2
CPAD = 64
NMOM = 4
NT = (((1,), (1,)), ((), ()))


def build_table():
    positions = np.arange(SEGLEN)
    harmonic = np.arange(1, SEGLEN // 2 + 1)
    phase = (positions[:, None] * harmonic[None, :] % SEGLEN) * (2.0 * math.pi / SEGLEN)
    window = 0.5 - 0.5 * np.cos(positions * (2.0 * math.pi / SEGLEN))
    table = np.concatenate([window[:, None] * np.cos(phase), window[:, None] * np.sin(phase)], axis=1)
    return table.astype(ml_dtypes.bfloat16)


def pair_table():
    columns = build_table().T
    even = np.pad(columns, ((0, 0), (0, SEGLEN)))
    odd = np.pad(columns, ((0, 0), (HALF, HALF)))
    return np.concatenate([even, odd], axis=0)


def split3(value):
    high = value.astype(jnp.bfloat16)
    rest = value - high.astype(jnp.float32)
    middle = rest.astype(jnp.bfloat16)
    low = (rest - middle.astype(jnp.float32)).astype(jnp.bfloat16)
    return high, middle, low


def moments_kernel(
    blocks, channels, tiles, labels, strain, table, influence, out, xs, even, odd, weights, parts
):
    block = pl.program_id(0)
    hotspots = influence.shape[1]
    freq_count = SEGLEN // 2

    @pl.when(block == 0)
    def _():
        xs[tiles * channels :, :] = jnp.zeros((xs.shape[0] - tiles * channels, LANES), jnp.float32)
        weights[...] = jnp.zeros_like(weights)
        for part in range(3):
            weights[part * CPAD : part * CPAD + channels, :] = influence[...]

    for tile in range(tiles):
        xs[tile * channels : (tile + 1) * channels, :] = strain[
            0, :, tile * LANES : (tile + 1) * LANES
        ].astype(jnp.float32)

    pair_rows = table[...]
    for pair in range(channels // 2):
        windows = []
        for channel in (2 * pair, 2 * pair + 1):
            here = xs[pl.ds(channel, LANES, stride=channels), :].astype(jnp.bfloat16)
            after = xs[pl.ds(channel + channels, LANES, stride=channels), :].astype(jnp.bfloat16)
            windows.append(jnp.concatenate([here, after], axis=1))
        window = jnp.concatenate(windows, axis=0)
        coeffs = lax.dot_general(pair_rows, window, NT, preferred_element_type=jnp.float32)
        for offset in range(2):
            channel = 2 * pair + offset
            lanes = slice(offset * LANES, (offset + 1) * LANES)
            even[pl.ds(channel, SEGLEN, stride=channels), :] = coeffs[:SEGLEN, lanes]
            odd[pl.ds(channel, SEGLEN, stride=channels), :] = coeffs[SEGLEN:, lanes]

    lane = lax.broadcasted_iota(jnp.int32, (1, LANES), 1)
    keep_odd = lane < tiles - 1
    first_half = lane < CPAD
    half_index = jnp.where(first_half, 1, 2).astype(jnp.float32)
    scale = 8.0 / (3.0 * SEGLEN * NSEG)
    totals = [jnp.zeros((channels, LANES), jnp.float32)] * NMOM
    gap = jnp.zeros((CPAD - channels, 4 * LANES), jnp.bfloat16)
    for pair in range(freq_count // 2):
        sides = []
        for freq in (2 * pair, 2 * pair + 1):
            pieces = []
            for line in (freq, freq + freq_count):
                rows = slice(line * channels, (line + 1) * channels)
                pieces.append(even[rows, :].astype(jnp.bfloat16))
                pieces.append(jnp.where(keep_odd, odd[rows, :], 0.0).astype(jnp.bfloat16))
            sides.append(jnp.concatenate(pieces, axis=1))
        left = jnp.concatenate(sides, axis=0)
        right = jnp.concatenate([sides[0], gap, sides[1], gap], axis=0)
        product = lax.dot_general(left, right, NT, preferred_element_type=jnp.float32)
        cospec = jnp.where(first_half, product[:channels], product[channels:]) * scale
        cospec = cospec.astype(jnp.bfloat16).astype(jnp.float32)
        frequency = (half_index + 2.0 * pair) * (1.0 / SEGLEN)
        square = frequency * frequency
        totals[0] = totals[0] + cospec
        totals[1] = totals[1] + cospec * frequency
        totals[2] = totals[2] + cospec * square
        totals[3] = totals[3] + cospec * (square * square)

    for moment in range(NMOM):
        whole = totals[moment] + pltpu.roll(totals[moment], CPAD, 1)
        high, middle, low = split3(whole * (1.0 / SEGLEN))
        start = pl.multiple_of((moment * blocks + block) * channels, 16)
        parts[pl.ds(start, channels), :LANES] = jnp.where(first_half, high, middle)
        parts[pl.ds(start, channels), LANES:] = low

    @pl.when(block == blocks - 1)
    def _():
        width = 2 * LANES
        for step in range(hotspots // width):
            lanes = slice(step * width, (step + 1) * width)
            column = influence[:, lanes].astype(jnp.float32)
            for moment in range(NMOM):
                rows = slice(moment * blocks * channels, (moment + 1) * blocks * channels)
                spread = jnp.dot(parts[rows, :], weights[:, lanes], preferred_element_type=jnp.float32)
                spread = spread.reshape(blocks, channels, width)
                value = jnp.sum(spread * column[None], axis=1)
                for half in range(2):
                    out[2 * step + half, moment] = value[:, half * LANES : (half + 1) * LANES]
        row = lax.broadcasted_iota(jnp.int32, (blocks, LANES), 0)
        named = jnp.zeros((blocks, LANES), jnp.float32)
        for index in range(blocks):
            label = (labels[0, index] * NDIR + labels[1, index]) * NYAW + labels[2, index]
            named = jnp.where(row == index, label.astype(jnp.float32), named)
        for step in range(hotspots // LANES):
            out[step, NMOM] = named


def local_moments(strain, bin_labels, influence):
    blocks, channels, samples = strain.shape
    hotspots = influence.shape[0]
    tiles = samples // LANES
    return pl.pallas_call(
        functools.partial(moments_kernel, blocks, channels, tiles),
        grid=(blocks,),
        in_specs=[
            pl.BlockSpec(memory_space=pltpu.SMEM),
            pl.BlockSpec((1, channels, samples), lambda b: (b, 0, 0)),
            pl.BlockSpec((2 * SEGLEN, 2 * SEGLEN), lambda b: (0, 0)),
            pl.BlockSpec((channels, hotspots), lambda b: (0, 0)),
        ],
        out_specs=pl.BlockSpec((hotspots // LANES, NMOM + 1, blocks, LANES), lambda b: (0, 0, 0, 0)),
        out_shape=jax.ShapeDtypeStruct((hotspots // LANES, NMOM + 1, blocks, LANES), jnp.float32),
        scratch_shapes=[
            pltpu.VMEM(((LANES + 1) * channels, LANES), jnp.float32),
            pltpu.VMEM((SEGLEN * channels, LANES), jnp.float32),
            pltpu.VMEM((SEGLEN * channels, LANES), jnp.float32),
            pltpu.VMEM((2 * LANES, hotspots), jnp.bfloat16),
            pltpu.VMEM((NMOM * blocks * channels, 2 * LANES), jnp.bfloat16),
        ],
        compiler_params=pltpu.CompilerParams(vmem_limit_bytes=48 << 20),
        name="block_moments",
    )(bin_labels.T, strain, jnp.asarray(pair_table()), influence.T)


def dirlik(moment_zero, moment_one, moment_two, moment_four):
    spread_ratio = moment_two / jnp.sqrt(moment_zero * moment_four)
    mean_freq = moment_one / moment_zero * jnp.sqrt(moment_two / moment_four)
    d_one = 2.0 * (mean_freq - spread_ratio**2) / (1.0 + spread_ratio**2)
    shared = 1.0 - spread_ratio - d_one + d_one**2
    r_ratio = (spread_ratio - mean_freq - d_one**2) / shared
    d_two = shared / (1.0 - r_ratio)
    d_three = 1.0 - d_one - d_two
    q_factor = 1.25 * (spread_ratio - d_three - d_two * r_ratio) / d_one
    peak_rate = jnp.sqrt(moment_four / moment_two)
    bracket = 6.0 * d_one * q_factor**3 + 2.8284271247 * 1.3293403882 * (
        jnp.abs(r_ratio) ** 3 * d_two + d_three
    )
    return peak_rate * (2.0 * jnp.sqrt(moment_zero)) ** 3 * bracket


def damage_kernel(received, damage, total):
    sources, _, blocks, width = received.shape
    count_blocks = sources * blocks
    named = received[:, NMOM].reshape(count_blocks, width)[:, :1]
    bins = lax.broadcasted_iota(jnp.int32, (count_blocks, NBIN), 1).astype(jnp.float32)
    member = jnp.where(named == bins, 1.0, 0.0)
    chosen = member.T.astype(jnp.bfloat16)
    count = jnp.sum(member.T, axis=1, keepdims=True)
    means = []
    for moment in range(NMOM):
        total_moment = jnp.zeros((NBIN, width), jnp.float32)
        for piece in split3(received[:, moment].reshape(count_blocks, width)):
            total_moment = total_moment + jnp.dot(chosen, piece, preferred_element_type=jnp.float32)
        means.append(total_moment / count)
    by_bin = dirlik(*means)
    damage[...] = by_bin
    total[...] = jnp.sum(count / count_blocks * by_bin, axis=0, keepdims=True)


def per_device(strain, bin_labels, influence):
    devices = lax.axis_size("tm")
    blocks = strain.shape[0]
    hotspots = influence.shape[0]
    width = hotspots // devices
    moments = local_moments(strain, bin_labels, influence)
    if width != LANES:
        share = LANES // width
        moments = moments.reshape(hotspots // LANES, NMOM + 1, blocks, share, width)
        moments = moments.transpose(0, 3, 1, 2, 4).reshape(devices, NMOM + 1, blocks, width)
    received = lax.all_to_all(moments, "tm", split_axis=0, concat_axis=0, tiled=True)
    damage, total = pl.pallas_call(
        damage_kernel,
        out_shape=(
            jax.ShapeDtypeStruct((NBIN, width), jnp.float32),
            jax.ShapeDtypeStruct((1, width), jnp.float32),
        ),
        name="bin_damage",
    )(received)
    return damage, total.reshape(width)


def solution(mesh):
    placed = (P(("groups", "tm"), None, None), P(("groups", "tm"), None), P())
    return jax.shard_map(
        per_device,
        mesh=mesh,
        in_specs=placed,
        out_specs=(P("groups", "tm"), P(("groups", "tm"))),
        check_vma=False,
    )
```

time: 119 us -> 69.1 us (0.58)
  Pallas kernels: 97.5 us -> 47.3 us
    pallas_call x1, Pallas kernels: 95.3 us -> 45.1 us  [local_moments(): pl.pallas_call(functools.partial(moments_kernel, blocks, channels, tiles)...]
    unnamed x2 -> x6, local copies, waits for them, and re-layouts: 1.96 us -> 2.5 us
where the time goes in v2:
time: 69.1 us; the launch traced here: 68.8 us
  Pallas kernels  47.3 us (68%)
  blocking collectives  18.4 us (27%)
  local copies, waits for them, and re-layouts  2.5 us (4%)
    pallas_call x1, Pallas kernels, local_moments(): pl.pallas_call(functools.partial(moments_kernel, blocks, channels, tiles)...  45.1 us
    all_to_all x1, blocking collectives, per_device(): lax.all_to_all(moments, 'tm', split_axis=0, concat_axis=0, tiled=True)  18.4 us
    unnamed x6, local copies, waits for them, and re-layouts  2.5 us
    pallas_call x1, Pallas kernels, per_device(): pl.pallas_call(damage_kernel, out_shape=(jax.ShapeDtypeStruct((NBIN, widt...  2.17 us

profile of v2, /device:TPU:0, one launch (start us, length us, event | category | flops | bytes accessed | tf_op | source)
XLA Modules:
  0.0 68.8 jit_solution(14361058002388687490)
XLA Ops:
  0.6 0.0 copy-start
  0.6 0.9 %copy-done = bf16[2048,48]{0,1:T(8,128)(2,1)S(1)} copy-done((bf16[2048,48]{0,1:T(8,128)(2,1)S(1)}, bf16[2048,48]{0,1:T(8,128)(2,1)}, u32[]{:S(2)}) %copy-start) | copy-done | bytes 196632
  1.6 0.0 copy-start.1
  1.6 0.9 %copy-done.1 = bf16[256,256]{1,0:T(8,128)(2,1)S(1)} copy-done((bf16[256,256]{1,0:T(8,128)(2,1)S(1)}, bf16[256,256]{1,0:T(8,128)(2,1)}, u32[]{:S(2)}) %copy-start.1) | copy-done | bytes 131096
  2.5 0.0 copy-start.2
  2.5 0.7 copy-done.2
  3.1 45.1 %block_moments.1 = f32[16,5,8,128]{3,2,1,0:T(8,128)S(1)} custom-call(s32[3,8]{1,0:T(4,128)S(1)} %bitcast.4, bf16[8,48,12032]{2,1,0:T(8,128)(2,1)} %strain.1, bf16[256,256]{1,0:T(8,128)(2,1)S(1)} %copy-done.1, bf16[48,2048]{1,0:T(8,128)(2,1)S(1)} %bitcast.3), custom_call_target="tpu_custom_call" | custom-call | tf_op jit(solution)/shard_map/block_moments/pallas_call | solution.py:144
  48.2 18.4 %all_to_all.5.received = f32[16,5,8,128]{3,2,1,0:T(8,128)} all-to-all(f32[16,5,8,128]{3,2,1,0:T(8,128)S(1)} %block_moments.1), channel_id=1, replica_groups=mesh['groups'=2,'tm'=16] {'tm'}, dimensions={0} | all-to-all | bytes 655360 | tf_op jit(solution)/shard_map/all_to_all | solution.py:212
  66.6 2.2 %bin_damage.1 = (f32[128,128]{1,0:T(8,128)}, f32[1,128]{1,0:T(1,128)}) custom-call(f32[16,5,8,128]{3,2,1,0:T(8,128)} %all_to_all.5.received), custom_call_target="tpu_custom_call" | custom-call | tf_op jit(solution)/shard_map/bin_damage/pallas_call | solution.py:213
Async XLA Ops:
  0.6 0.9 %copy-start = (bf16[2048,48]{0,1:T(8,128)(2,1)S(1)}, bf16[2048,48]{0,1:T(8,128)(2,1)}, u32[]{:S(2)}) copy-start(bf16[2048,48]{0,1:T(8,128)(2,1)} %param.6) | copy-start | bytes 589828
  1.6 0.9 %copy-start.1 = (bf16[256,256]{1,0:T(8,128)(2,1)S(1)}, bf16[256,256]{1,0:T(8,128)(2,1)}, u32[]{:S(2)}) copy-start(bf16[256,256]{1,0:T(8,128)(2,1)} %constant.2.clone.table) | copy-start | bytes 393220
  2.5 0.7 copy-start.2

commit v3 on v2

--- a/solution.py
+++ b/solution.py
@@ -19,6 +19,8 @@
 HALF = SEGLEN // 2
 CPAD = 64
 NMOM = 4
+WINDOWS = 96
+STRIDE = 49
 NT = (((1,), (1,)), ((), ()))
 
 
@@ -55,50 +57,50 @@
 
     @pl.when(block == 0)
     def _():
-        xs[tiles * channels :, :] = jnp.zeros((xs.shape[0] - tiles * channels, LANES), jnp.float32)
+        xs[tiles * STRIDE :, :] = jnp.zeros((xs.shape[0] - tiles * STRIDE, LANES), jnp.float32)
         weights[...] = jnp.zeros_like(weights)
         for part in range(3):
             weights[part * CPAD : part * CPAD + channels, :] = influence[...]
 
     for tile in range(tiles):
-        xs[tile * channels : (tile + 1) * channels, :] = strain[
+        xs[tile * STRIDE : tile * STRIDE + channels, :] = strain[
             0, :, tile * LANES : (tile + 1) * LANES
         ].astype(jnp.float32)
 
     pair_rows = table[...]
+    spare = jnp.zeros((LANES - WINDOWS, 2 * LANES), jnp.bfloat16)
     for pair in range(channels // 2):
         windows = []
         for channel in (2 * pair, 2 * pair + 1):
-            here = xs[pl.ds(channel, LANES, stride=channels), :].astype(jnp.bfloat16)
-            after = xs[pl.ds(channel + channels, LANES, stride=channels), :].astype(jnp.bfloat16)
-            windows.append(jnp.concatenate([here, after], axis=1))
+            here = xs[pl.ds(channel, WINDOWS, stride=STRIDE), :].astype(jnp.bfloat16)
+            after = xs[pl.ds(channel + STRIDE, WINDOWS, stride=STRIDE), :].astype(jnp.bfloat16)
+            windows += [jnp.concatenate([here, after], axis=1), spare]
         window = jnp.concatenate(windows, axis=0)
         coeffs = lax.dot_general(pair_rows, window, NT, preferred_element_type=jnp.float32)
         for offset in range(2):
             channel = 2 * pair + offset
             lanes = slice(offset * LANES, (offset + 1) * LANES)
-            even[pl.ds(channel, SEGLEN, stride=channels), :] = coeffs[:SEGLEN, lanes]
-            odd[pl.ds(channel, SEGLEN, stride=channels), :] = coeffs[SEGLEN:, lanes]
+            even[pl.ds(channel, SEGLEN, stride=STRIDE), :] = coeffs[:SEGLEN, lanes]
+            odd[pl.ds(channel, SEGLEN, stride=STRIDE), :] = coeffs[SEGLEN:, lanes]
 
     lane = lax.broadcasted_iota(jnp.int32, (1, LANES), 1)
     keep_odd = lane < tiles - 1
-    first_half = lane < CPAD
+    first_half = lane[:, : 2 * channels] < channels
     half_index = jnp.where(first_half, 1, 2).astype(jnp.float32)
     scale = 8.0 / (3.0 * SEGLEN * NSEG)
-    totals = [jnp.zeros((channels, LANES), jnp.float32)] * NMOM
-    gap = jnp.zeros((CPAD - channels, 4 * LANES), jnp.bfloat16)
+
+    totals = [jnp.zeros((channels, 2 * channels), jnp.float32)] * NMOM
     for pair in range(freq_count // 2):
         sides = []
         for freq in (2 * pair, 2 * pair + 1):
             pieces = []
             for line in (freq, freq + freq_count):
-                rows = slice(line * channels, (line + 1) * channels)
+                rows = slice(line * STRIDE, line * STRIDE + channels)
                 pieces.append(even[rows, :].astype(jnp.bfloat16))
-                pieces.append(jnp.where(keep_odd, odd[rows, :], 0.0).astype(jnp.bfloat16))
+                pieces.append(jnp.where(keep_odd, odd[rows, :].astype(jnp.bfloat16), jnp.bfloat16(0)))
             sides.append(jnp.concatenate(pieces, axis=1))
-        left = jnp.concatenate(sides, axis=0)
-        right = jnp.concatenate([sides[0], gap, sides[1], gap], axis=0)
-        product = lax.dot_general(left, right, NT, preferred_element_type=jnp.float32)
+        both = jnp.concatenate(sides, axis=0)
+        product = lax.dot_general(both, both, NT, preferred_element_type=jnp.float32)
         cospec = jnp.where(first_half, product[:channels], product[channels:]) * scale
         cospec = cospec.astype(jnp.bfloat16).astype(jnp.float32)
         frequency = (half_index + 2.0 * pair) * (1.0 / SEGLEN)
@@ -109,10 +111,11 @@
         totals[3] = totals[3] + cospec * (square * square)
 
     for moment in range(NMOM):
-        whole = totals[moment] + pltpu.roll(totals[moment], CPAD, 1)
-        high, middle, low = split3(whole * (1.0 / SEGLEN))
+        whole = (totals[moment][:, :channels] + totals[moment][:, channels:]) * (1.0 / SEGLEN)
+        whole = jnp.concatenate([whole, jnp.zeros((channels, CPAD - channels), jnp.float32)] * 2, axis=1)
+        high, middle, low = split3(whole)
         start = pl.multiple_of((moment * blocks + block) * channels, 16)
-        parts[pl.ds(start, channels), :LANES] = jnp.where(first_half, high, middle)
+        parts[pl.ds(start, channels), :LANES] = jnp.where(lane < CPAD, high, middle)
         parts[pl.ds(start, channels), LANES:] = low
 
     @pl.when(block == blocks - 1)
@@ -153,13 +156,13 @@
         out_specs=pl.BlockSpec((hotspots // LANES, NMOM + 1, blocks, LANES), lambda b: (0, 0, 0, 0)),
         out_shape=jax.ShapeDtypeStruct((hotspots // LANES, NMOM + 1, blocks, LANES), jnp.float32),
         scratch_shapes=[
-            pltpu.VMEM(((LANES + 1) * channels, LANES), jnp.float32),
-            pltpu.VMEM((SEGLEN * channels, LANES), jnp.float32),
-            pltpu.VMEM((SEGLEN * channels, LANES), jnp.float32),
+            pltpu.VMEM(((LANES + 1) * STRIDE, LANES), jnp.float32),
+            pltpu.VMEM((SEGLEN * STRIDE, LANES), jnp.float32),
+            pltpu.VMEM((SEGLEN * STRIDE, LANES), jnp.float32),
             pltpu.VMEM((2 * LANES, hotspots), jnp.bfloat16),
             pltpu.VMEM((NMOM * blocks * channels, 2 * LANES), jnp.bfloat16),
         ],
-        compiler_params=pltpu.CompilerParams(vmem_limit_bytes=48 << 20),
+        compiler_params=pltpu.CompilerParams(vmem_limit_bytes=60 << 20),
         name="block_moments",
     )(bin_labels.T, strain, jnp.asarray(pair_table()), influence.T)
 

time: 69.1 us -> 43.2 us (0.63)
  Pallas kernels: 47.3 us -> 23.7 us
  local copies, waits for them, and re-layouts: 2.5 us -> 0 us
    pallas_call x1, Pallas kernels: 45.1 us -> 21.6 us  [local_moments(): pl.pallas_call(functools.partial(moments_kernel, blocks, channels, tiles)...]
    unnamed x6 -> x0, local copies, waits for them, and re-layouts: 2.5 us -> none
where the time goes in v3:
time: 43.2 us; the launch traced here: 43 us
  Pallas kernels  23.7 us (55%)
  blocking collectives  18.6 us (43%)
  between operations  0.63 us (1%)
    pallas_call x1, Pallas kernels, local_moments(): pl.pallas_call(functools.partial(moments_kernel, blocks, channels, tiles)...  21.6 us
    all_to_all x1, blocking collectives, per_device(): lax.all_to_all(moments, 'tm', split_axis=0, concat_axis=0, tiled=True)  18.6 us
    pallas_call x1, Pallas kernels, per_device(): pl.pallas_call(damage_kernel, out_shape=(jax.ShapeDtypeStruct((NBIN, widt...  2.17 us

profile of v3, /device:TPU:0, one launch (start us, length us, event | category | flops | bytes accessed | tf_op | source)
XLA Modules:
  0.0 43.0 jit_solution(16197843754362665168)
XLA Ops:
  0.6 21.6 %block_moments.1 = f32[16,5,8,128]{3,2,1,0:T(8,128)} custom-call(s32[3,8]{1,0:T(4,128)} %bitcast.4, bf16[8,48,12032]{2,1,0:T(8,128)(2,1)} %strain.1, bf16[256,256]{1,0:T(8,128)(2,1)} %constant.2.clone.table, bf16[48,2048]{1,0:T(8,128)(2,1)} %bitcast.3), custom_call_target="tpu_custom_call" | custom-call | tf_op jit(solution)/shard_map/block_moments/pallas_call | solution.py:147
  22.2 18.6 %all_to_all.5.received = f32[16,5,8,128]{3,2,1,0:T(8,128)} all-to-all(f32[16,5,8,128]{3,2,1,0:T(8,128)} %block_moments.1), channel_id=1, replica_groups=mesh['groups'=2,'tm'=16] {'tm'}, dimensions={0} | all-to-all | bytes 655360 | tf_op jit(solution)/shard_map/all_to_all | solution.py:215
  40.8 2.2 %bin_damage.1 = (f32[128,128]{1,0:T(8,128)}, f32[1,128]{1,0:T(1,128)}) custom-call(f32[16,5,8,128]{3,2,1,0:T(8,128)} %all_to_all.5.received), custom_call_target="tpu_custom_call" | custom-call | tf_op jit(solution)/shard_map/bin_damage/pallas_call | solution.py:216

commit v4 on v3

--- a/solution.py
+++ b/solution.py
@@ -49,7 +49,7 @@
 
 
 def moments_kernel(
-    blocks, channels, tiles, labels, strain, table, influence, out, xs, even, odd, weights, parts
+    blocks, channels, tiles, damages, labels, strain, table, influence, out, xs, even, odd, weights, parts
 ):
     block = pl.program_id(0)
     hotspots = influence.shape[1]
@@ -124,28 +124,36 @@
         for step in range(hotspots // width):
             lanes = slice(step * width, (step + 1) * width)
             column = influence[:, lanes].astype(jnp.float32)
+            values = []
             for moment in range(NMOM):
                 rows = slice(moment * blocks * channels, (moment + 1) * blocks * channels)
                 spread = jnp.dot(parts[rows, :], weights[:, lanes], preferred_element_type=jnp.float32)
                 spread = spread.reshape(blocks, channels, width)
-                value = jnp.sum(spread * column[None], axis=1)
-                for half in range(2):
-                    out[2 * step + half, moment] = value[:, half * LANES : (half + 1) * LANES]
-        row = lax.broadcasted_iota(jnp.int32, (blocks, LANES), 0)
-        named = jnp.zeros((blocks, LANES), jnp.float32)
+                values.append(jnp.sum(spread * column[None], axis=1))
+            if damages:
+                values = [dirlik(*values)]
+            for half in range(2):
+                start = (2 * step + half) * out.shape[0] // (hotspots // LANES)
+                for value in values:
+                    out[start : start + blocks, :] = value[:, half * LANES : (half + 1) * LANES]
+                    start += blocks
+        lanes = lax.broadcasted_iota(jnp.int32, (1, LANES), 1)
+        named = jnp.zeros((1, LANES), jnp.float32)
         for index in range(blocks):
             label = (labels[0, index] * NDIR + labels[1, index]) * NYAW + labels[2, index]
-            named = jnp.where(row == index, label.astype(jnp.float32), named)
+            named = jnp.where(lanes % blocks == index, label.astype(jnp.float32), named)
+        part = out.shape[0] // (hotspots // LANES)
         for step in range(hotspots // LANES):
-            out[step, NMOM] = named
-
-
-def local_moments(strain, bin_labels, influence):
+            out[(step + 1) * part - 1 : (step + 1) * part, :] = named
+
+
+def local_rows(strain, bin_labels, influence, damages):
     blocks, channels, samples = strain.shape
     hotspots = influence.shape[0]
     tiles = samples // LANES
+    rows = ((1 if damages else NMOM) * blocks + 1) * (hotspots // LANES)
     return pl.pallas_call(
-        functools.partial(moments_kernel, blocks, channels, tiles),
+        functools.partial(moments_kernel, blocks, channels, tiles, damages),
         grid=(blocks,),
         in_specs=[
             pl.BlockSpec(memory_space=pltpu.SMEM),
@@ -153,10 +161,10 @@
             pl.BlockSpec((2 * SEGLEN, 2 * SEGLEN), lambda b: (0, 0)),
             pl.BlockSpec((channels, hotspots), lambda b: (0, 0)),
         ],
-        out_specs=pl.BlockSpec((hotspots // LANES, NMOM + 1, blocks, LANES), lambda b: (0, 0, 0, 0)),
-        out_shape=jax.ShapeDtypeStruct((hotspots // LANES, NMOM + 1, blocks, LANES), jnp.float32),
+        out_specs=pl.BlockSpec((rows, LANES), lambda b: (0, 0)),
+        out_shape=jax.ShapeDtypeStruct((rows, LANES), jnp.float32),
         scratch_shapes=[
-            pltpu.VMEM(((LANES + 1) * STRIDE, LANES), jnp.float32),
+            pltpu.VMEM(((WINDOWS + 1) * STRIDE, LANES), jnp.float32),
             pltpu.VMEM((SEGLEN * STRIDE, LANES), jnp.float32),
             pltpu.VMEM((SEGLEN * STRIDE, LANES), jnp.float32),
             pltpu.VMEM((2 * LANES, hotspots), jnp.bfloat16),
@@ -183,18 +191,38 @@
     return peak_rate * (2.0 * jnp.sqrt(moment_zero)) ** 3 * bracket
 
 
-def damage_kernel(received, damage, total):
-    sources, _, blocks, width = received.shape
-    count_blocks = sources * blocks
-    named = received[:, NMOM].reshape(count_blocks, width)[:, :1]
-    bins = lax.broadcasted_iota(jnp.int32, (count_blocks, NBIN), 1).astype(jnp.float32)
-    member = jnp.where(named == bins, 1.0, 0.0)
-    chosen = member.T.astype(jnp.bfloat16)
-    count = jnp.sum(member.T, axis=1, keepdims=True)
+def gather_kernel(sources, received, damage, total):
+    count_blocks, width = damage.shape
+    blocks = count_blocks // sources
+    part = blocks + 1
+    by_block = jnp.concatenate(
+        [received[source * part : source * part + blocks, :] for source in range(sources)], axis=0
+    )
+    named = jnp.concatenate(
+        [received[(source + 1) * part - 1 : (source + 1) * part, :] for source in range(sources)], axis=0
+    )
+    source = lax.broadcasted_iota(jnp.int32, named.shape, 0)
+    lane = lax.broadcasted_iota(jnp.int32, named.shape, 1)
+    named = jnp.sum(jnp.where(lane // blocks == source, named, 0.0), axis=0, keepdims=True)
+    bins = lax.broadcasted_iota(jnp.int32, (NBIN, count_blocks), 0).astype(jnp.float32)
+    chosen = jnp.where(named == bins, 1.0, 0.0).astype(jnp.bfloat16)
+    by_bin = jnp.zeros((NBIN, width), jnp.float32)
+    for piece in split3(by_block):
+        by_bin = by_bin + jnp.dot(chosen, piece, preferred_element_type=jnp.float32)
+    damage[...] = by_bin
+    total[...] = jnp.sum(by_block * (1.0 / count_blocks), axis=0, keepdims=True)
+
+
+def bin_kernel(named, moments, damage, total):
+    count_blocks = named.shape[1]
+    bins = lax.broadcasted_iota(jnp.int32, (NBIN, count_blocks), 0).astype(jnp.float32)
+    member = jnp.where(named[...] == bins, 1.0, 0.0)
+    count = jnp.sum(member, axis=1, keepdims=True)
+    chosen = member.astype(jnp.bfloat16)
     means = []
     for moment in range(NMOM):
-        total_moment = jnp.zeros((NBIN, width), jnp.float32)
-        for piece in split3(received[:, moment].reshape(count_blocks, width)):
+        total_moment = jnp.zeros(damage.shape, jnp.float32)
+        for piece in split3(moments[moment]):
             total_moment = total_moment + jnp.dot(chosen, piece, preferred_element_type=jnp.float32)
         means.append(total_moment / count)
     by_bin = dirlik(*means)
@@ -207,20 +235,30 @@
     blocks = strain.shape[0]
     hotspots = influence.shape[0]
     width = hotspots // devices
-    moments = local_moments(strain, bin_labels, influence)
-    if width != LANES:
-        share = LANES // width
-        moments = moments.reshape(hotspots // LANES, NMOM + 1, blocks, share, width)
-        moments = moments.transpose(0, 3, 1, 2, 4).reshape(devices, NMOM + 1, blocks, width)
-    received = lax.all_to_all(moments, "tm", split_axis=0, concat_axis=0, tiled=True)
-    damage, total = pl.pallas_call(
-        damage_kernel,
-        out_shape=(
-            jax.ShapeDtypeStruct((NBIN, width), jnp.float32),
-            jax.ShapeDtypeStruct((1, width), jnp.float32),
-        ),
-        name="bin_damage",
-    )(received)
+    out_shape = (
+        jax.ShapeDtypeStruct((NBIN, width), jnp.float32),
+        jax.ShapeDtypeStruct((1, width), jnp.float32),
+    )
+    if blocks * devices == NBIN and width == LANES:
+        rows = local_rows(strain, bin_labels, influence, True)
+        rows = rows.reshape(devices, 1, (blocks + 1) * LANES)
+        received = lax.all_to_all(rows, "tm", split_axis=0, concat_axis=0, tiled=True)
+        damage, total = pl.pallas_call(
+            functools.partial(gather_kernel, devices), out_shape=out_shape, name="gather_damage"
+        )(received.reshape(devices * (blocks + 1), LANES))
+        return damage, total.reshape(width)
+    rows = local_rows(strain, bin_labels, influence, False)
+    rows = rows.reshape(hotspots // LANES, NMOM * blocks + 1, LANES)
+    named = jnp.broadcast_to(rows[:1, -1, :blocks], (devices, blocks))
+    moments = rows[:, :-1].reshape(hotspots // LANES, NMOM, blocks, LANES)
+    moments = moments.transpose(1, 2, 0, 3).reshape(NMOM, blocks, devices, width)
+    moments = moments.transpose(2, 0, 1, 3).reshape(devices, NMOM * blocks * width)
+    sent = jnp.concatenate([moments, named], axis=1)
+    received = lax.all_to_all(sent, "tm", split_axis=0, concat_axis=0, tiled=True)
+    named = received[:, -blocks:].reshape(1, devices * blocks)
+    moments = received[:, :-blocks].reshape(devices, NMOM, blocks, width)
+    moments = moments.transpose(1, 0, 2, 3).reshape(NMOM, devices * blocks, width)
+    damage, total = pl.pallas_call(bin_kernel, out_shape=out_shape, name="bin_damage")(named, moments)
     return damage, total.reshape(width)
 
 

time: 43.2 us -> 40.2 us (0.931)
  blocking collectives: 18.6 us -> 14.5 us
  Pallas kernels: 23.7 us -> 24.8 us
    all_to_all x1, blocking collectives: 18.6 us -> 14.5 us  [per_device(): lax.all_to_all(rows, 'tm', split_axis=0, concat_axis=0, tiled=True)]
    pallas_call x2, Pallas kernels: 23.7 us -> 24.8 us  [the longest x1 23.1 us: local_rows(): pl.pallas_call(functools.partial(moments_kernel, blocks, channels, tiles,...]
where the time goes in v4:
time: 40.2 us; the launch traced here: 39.9 us
  Pallas kernels  24.8 us (62%)
  blocking collectives  14.5 us (36%)
  between operations  0.63 us (2%)
    pallas_call x1, Pallas kernels, local_rows(): pl.pallas_call(functools.partial(moments_kernel, blocks, channels, tiles,...  23.1 us
    all_to_all x1, blocking collectives, per_device(): lax.all_to_all(rows, 'tm', split_axis=0, concat_axis=0, tiled=True)  14.5 us
    pallas_call x1, Pallas kernels, per_device(): pl.pallas_call(functools.partial(gather_kernel, devices), out_shape=out_s...  1.69 us

profile of v4, /device:TPU:0, one launch (start us, length us, event | category | flops | bytes accessed | tf_op | source)
XLA Modules:
  0.0 39.9 jit_solution(2296300278522966908)
XLA Ops:
  0.6 23.1 %block_moments.1 = f32[144,128]{1,0:T(8,128)} custom-call(s32[3,8]{1,0:T(4,128)} %bitcast.8, bf16[8,48,12032]{2,1,0:T(8,128)(2,1)} %strain.1, bf16[256,256]{1,0:T(8,128)(2,1)} %constant.2.clone.table, bf16[48,2048]{1,0:T(8,128)(2,1)} %bitcast.7), custom_call_target="tpu_custom_call" | custom-call | tf_op jit(solution)/shard_map/block_moments/pallas_call | solution.py:155
  23.7 14.5 %all_to_all.5 = f32[16,1,1152]{2,1,0:T(1,128)} all-to-all(f32[16,1,1152]{2,1,0:T(1,128)} %bitcast.5), channel_id=1, replica_groups=mesh['groups'=2,'tm'=16] {'tm'}, dimensions={0} | all-to-all | bytes 147456 | tf_op jit(solution)/shard_map/all_to_all | solution.py:245
  38.2 1.7 %gather_damage.1 = (f32[128,128]{1,0:T(8,128)}, f32[1,128]{1,0:T(1,128)}) custom-call(f32[144,128]{1,0:T(8,128)} %bitcast.6), custom_call_target="tpu_custom_call" | custom-call | tf_op jit(solution)/shard_map/gather_damage/pallas_call | solution.py:246

commit v5 on v4

--- a/solution.py
+++ b/solution.py
@@ -21,6 +21,8 @@
 NMOM = 4
 WINDOWS = 96
 STRIDE = 49
+XSHARE = 0
+GROUP = 2
 NT = (((1,), (1,)), ((), ()))
 
 
@@ -48,101 +50,136 @@
     return high, middle, low
 
 
+def spread_samples(strain, xs, tile):
+    channels = strain.shape[1]
+    xs[tile * STRIDE : tile * STRIDE + channels, :] = strain[
+        0, :, tile * LANES : (tile + 1) * LANES
+    ].astype(jnp.float32)
+
+
+def transform(table, xs, even, odd, pair):
+    spare = jnp.zeros((LANES - WINDOWS, 2 * LANES), jnp.bfloat16)
+    windows = []
+    for channel in (2 * pair, 2 * pair + 1):
+        here = xs[pl.ds(channel, WINDOWS, stride=STRIDE), :].astype(jnp.bfloat16)
+        after = xs[pl.ds(channel + STRIDE, WINDOWS, stride=STRIDE), :].astype(jnp.bfloat16)
+        windows += [jnp.concatenate([here, after], axis=1), spare]
+    window = jnp.concatenate(windows, axis=0)
+    coeffs = lax.dot_general(table[...], window, NT, preferred_element_type=jnp.float32)
+    for offset in range(2):
+        channel = 2 * pair + offset
+        lanes = slice(offset * LANES, (offset + 1) * LANES)
+        even[pl.ds(channel, SEGLEN, stride=STRIDE), :] = coeffs[:SEGLEN, lanes]
+        odd[pl.ds(channel, SEGLEN, stride=STRIDE), :] = coeffs[SEGLEN:, lanes]
+
+
+def add_cross(channels, keep_odd, even, odd, pair, totals):
+    freq_count = SEGLEN // 2
+    sides = []
+    for freq in (2 * pair, 2 * pair + 1):
+        pieces = []
+        for line in (freq, freq + freq_count):
+            rows = slice(line * STRIDE, line * STRIDE + channels)
+            pieces.append(even[rows, :].astype(jnp.bfloat16))
+            pieces.append(jnp.where(keep_odd, odd[rows, :].astype(jnp.bfloat16), jnp.bfloat16(0)))
+        sides.append(jnp.concatenate(pieces, axis=1))
+    both = jnp.concatenate(sides, axis=0)
+    product = lax.dot_general(both, both, NT, preferred_element_type=jnp.float32)
+    first_half = lax.broadcasted_iota(jnp.int32, (1, 2 * channels), 1) < channels
+    scale = 8.0 / (3.0 * SEGLEN * NSEG)
+    cospec = jnp.where(first_half, product[:channels], product[channels:]) * scale
+    cospec = cospec.astype(jnp.bfloat16).astype(jnp.float32)
+    frequency = jnp.where(first_half, (2 * pair + 1) / SEGLEN, (2 * pair + 2) / SEGLEN)
+    square = frequency * frequency
+    totals[0] = totals[0] + cospec
+    totals[1] = totals[1] + cospec * frequency
+    totals[2] = totals[2] + cospec * square
+    totals[3] = totals[3] + cospec * (square * square)
+
+
 def moments_kernel(
-    blocks, channels, tiles, damages, labels, strain, table, influence, out, xs, even, odd, weights, parts
+    blocks, channels, tiles, damages, labels, strain, table, influence, out, xs, even0, odd0, even1, odd1, weights, parts
 ):
-    block = pl.program_id(0)
+    step_index = pl.program_id(0)
     hotspots = influence.shape[1]
-    freq_count = SEGLEN // 2
-
-    @pl.when(block == 0)
+    pairs = channels // 2
+    lines = SEGLEN // 4
+    slots = ((even0, odd0), (even1, odd1))
+    lane = lax.broadcasted_iota(jnp.int32, (1, LANES), 1)
+    keep_odd = lane < tiles - 1
+
+    def work(source, target):
+        totals = [jnp.zeros((channels, 2 * channels), jnp.float32)] * NMOM
+        done = 0
+
+        def catch_up(goal):
+            nonlocal done
+            while source is not None and done < min(goal, lines):
+                add_cross(channels, keep_odd, *slots[source], done, totals)
+                done += 1
+
+        if target is not None:
+            for tile in range(tiles):
+                spread_samples(strain, xs, tile)
+                catch_up((tile + 1) * XSHARE // tiles)
+            for pair in range(pairs):
+                transform(table, xs, *slots[target], pair)
+                catch_up(XSHARE + (pair + 1) * (lines - XSHARE) // pairs)
+        catch_up(lines)
+        if source is None:
+            return
+        block = step_index - 1
+        for moment in range(NMOM):
+            whole = (totals[moment][:, :channels] + totals[moment][:, channels:]) * (1.0 / SEGLEN)
+            gap = jnp.zeros((channels, CPAD - channels), jnp.float32)
+            high, middle, low = split3(jnp.concatenate([whole, gap] * 2, axis=1))
+            start = pl.multiple_of((moment * blocks + block) * channels, 16)
+            parts[pl.ds(start, channels), :LANES] = jnp.where(lane < CPAD, high, middle)
+            parts[pl.ds(start, channels), LANES:] = low
+
+    @pl.when(step_index == 0)
     def _():
         xs[tiles * STRIDE :, :] = jnp.zeros((xs.shape[0] - tiles * STRIDE, LANES), jnp.float32)
         weights[...] = jnp.zeros_like(weights)
         for part in range(3):
             weights[part * CPAD : part * CPAD + channels, :] = influence[...]
-
-    for tile in range(tiles):
-        xs[tile * STRIDE : tile * STRIDE + channels, :] = strain[
-            0, :, tile * LANES : (tile + 1) * LANES
-        ].astype(jnp.float32)
-
-    pair_rows = table[...]
-    spare = jnp.zeros((LANES - WINDOWS, 2 * LANES), jnp.bfloat16)
-    for pair in range(channels // 2):
-        windows = []
-        for channel in (2 * pair, 2 * pair + 1):
-            here = xs[pl.ds(channel, WINDOWS, stride=STRIDE), :].astype(jnp.bfloat16)
-            after = xs[pl.ds(channel + STRIDE, WINDOWS, stride=STRIDE), :].astype(jnp.bfloat16)
-            windows += [jnp.concatenate([here, after], axis=1), spare]
-        window = jnp.concatenate(windows, axis=0)
-        coeffs = lax.dot_general(pair_rows, window, NT, preferred_element_type=jnp.float32)
-        for offset in range(2):
-            channel = 2 * pair + offset
-            lanes = slice(offset * LANES, (offset + 1) * LANES)
-            even[pl.ds(channel, SEGLEN, stride=STRIDE), :] = coeffs[:SEGLEN, lanes]
-            odd[pl.ds(channel, SEGLEN, stride=STRIDE), :] = coeffs[SEGLEN:, lanes]
-
-    lane = lax.broadcasted_iota(jnp.int32, (1, LANES), 1)
-    keep_odd = lane < tiles - 1
-    first_half = lane[:, : 2 * channels] < channels
-    half_index = jnp.where(first_half, 1, 2).astype(jnp.float32)
-    scale = 8.0 / (3.0 * SEGLEN * NSEG)
-
-    totals = [jnp.zeros((channels, 2 * channels), jnp.float32)] * NMOM
-    for pair in range(freq_count // 2):
-        sides = []
-        for freq in (2 * pair, 2 * pair + 1):
-            pieces = []
-            for line in (freq, freq + freq_count):
-                rows = slice(line * STRIDE, line * STRIDE + channels)
-                pieces.append(even[rows, :].astype(jnp.bfloat16))
-                pieces.append(jnp.where(keep_odd, odd[rows, :].astype(jnp.bfloat16), jnp.bfloat16(0)))
-            sides.append(jnp.concatenate(pieces, axis=1))
-        both = jnp.concatenate(sides, axis=0)
-        product = lax.dot_general(both, both, NT, preferred_element_type=jnp.float32)
-        cospec = jnp.where(first_half, product[:channels], product[channels:]) * scale
-        cospec = cospec.astype(jnp.bfloat16).astype(jnp.float32)
-        frequency = (half_index + 2.0 * pair) * (1.0 / SEGLEN)
-        square = frequency * frequency
-        totals[0] = totals[0] + cospec
-        totals[1] = totals[1] + cospec * frequency
-        totals[2] = totals[2] + cospec * square
-        totals[3] = totals[3] + cospec * (square * square)
-
-    for moment in range(NMOM):
-        whole = (totals[moment][:, :channels] + totals[moment][:, channels:]) * (1.0 / SEGLEN)
-        whole = jnp.concatenate([whole, jnp.zeros((channels, CPAD - channels), jnp.float32)] * 2, axis=1)
-        high, middle, low = split3(whole)
-        start = pl.multiple_of((moment * blocks + block) * channels, 16)
-        parts[pl.ds(start, channels), :LANES] = jnp.where(lane < CPAD, high, middle)
-        parts[pl.ds(start, channels), LANES:] = low
-
-    @pl.when(block == blocks - 1)
+        work(None, 0)
+
+    for parity in range(2):
+
+        @pl.when((step_index > 0) & (step_index < blocks) & (step_index % 2 == parity))
+        def _():
+            work(1 - parity, parity)
+
+    @pl.when(step_index == blocks)
     def _():
+        work((blocks - 1) % 2, None)
         width = 2 * LANES
-        for step in range(hotspots // width):
-            lanes = slice(step * width, (step + 1) * width)
-            column = influence[:, lanes].astype(jnp.float32)
+        count = hotspots // width
+        part = out.shape[0] // (hotspots // LANES)
+        for first in range(0, count, GROUP):
             values = []
             for moment in range(NMOM):
                 rows = slice(moment * blocks * channels, (moment + 1) * blocks * channels)
-                spread = jnp.dot(parts[rows, :], weights[:, lanes], preferred_element_type=jnp.float32)
-                spread = spread.reshape(blocks, channels, width)
-                values.append(jnp.sum(spread * column[None], axis=1))
+                values.append([])
+                for step in range(first, first + GROUP):
+                    lanes = slice(step * width, (step + 1) * width)
+                    column = influence[:, lanes].astype(jnp.float32)
+                    spread = jnp.dot(parts[rows, :], weights[:, lanes], preferred_element_type=jnp.float32)
+                    spread = spread.reshape(blocks, channels, width)
+                    values[-1].append(jnp.sum(spread * column[None], axis=1))
+            values = [jnp.concatenate(value, axis=1) for value in values]
             if damages:
                 values = [dirlik(*values)]
-            for half in range(2):
-                start = (2 * step + half) * out.shape[0] // (hotspots // LANES)
+            for half in range(2 * GROUP):
+                start = (2 * first + half) * part
                 for value in values:
                     out[start : start + blocks, :] = value[:, half * LANES : (half + 1) * LANES]
                     start += blocks
-        lanes = lax.broadcasted_iota(jnp.int32, (1, LANES), 1)
         named = jnp.zeros((1, LANES), jnp.float32)
         for index in range(blocks):
             label = (labels[0, index] * NDIR + labels[1, index]) * NYAW + labels[2, index]
-            named = jnp.where(lanes % blocks == index, label.astype(jnp.float32), named)
-        part = out.shape[0] // (hotspots // LANES)
+            named = jnp.where(lane % blocks == index, label.astype(jnp.float32), named)
         for step in range(hotspots // LANES):
             out[(step + 1) * part - 1 : (step + 1) * part, :] = named
 
@@ -154,10 +191,10 @@
     rows = ((1 if damages else NMOM) * blocks + 1) * (hotspots // LANES)
     return pl.pallas_call(
         functools.partial(moments_kernel, blocks, channels, tiles, damages),
-        grid=(blocks,),
+        grid=(blocks + 1,),
         in_specs=[
             pl.BlockSpec(memory_space=pltpu.SMEM),
-            pl.BlockSpec((1, channels, samples), lambda b: (b, 0, 0)),
+            pl.BlockSpec((1, channels, samples), lambda b: (jnp.minimum(b, blocks - 1), 0, 0)),
             pl.BlockSpec((2 * SEGLEN, 2 * SEGLEN), lambda b: (0, 0)),
             pl.BlockSpec((channels, hotspots), lambda b: (0, 0)),
         ],
@@ -165,8 +202,7 @@
         out_shape=jax.ShapeDtypeStruct((rows, LANES), jnp.float32),
         scratch_shapes=[
             pltpu.VMEM(((WINDOWS + 1) * STRIDE, LANES), jnp.float32),
-            pltpu.VMEM((SEGLEN * STRIDE, LANES), jnp.float32),
-            pltpu.VMEM((SEGLEN * STRIDE, LANES), jnp.float32),
+            *[pltpu.VMEM((SEGLEN * STRIDE, LANES), jnp.float32)] * 4,
             pltpu.VMEM((2 * LANES, hotspots), jnp.bfloat16),
             pltpu.VMEM((NMOM * blocks * channels, 2 * LANES), jnp.bfloat16),
         ],

time: 40.2 us -> 37.8 us (0.940)
  Pallas kernels: 24.8 us -> 22.4 us
    pallas_call x1, Pallas kernels: 23.1 us -> 20.7 us  [local_rows(): pl.pallas_call(functools.partial(moments_kernel, blocks, channels, tiles,...]
where the time goes in v5:
time: 37.8 us; the launch traced here: 37.5 us
  Pallas kernels  22.4 us (59%)
  blocking collectives  14.5 us (38%)
  between operations  0.63 us (2%)
    pallas_call x1, Pallas kernels, local_rows(): pl.pallas_call(functools.partial(moments_kernel, blocks, channels, tiles,...  20.7 us
    all_to_all x1, blocking collectives, per_device(): lax.all_to_all(rows, 'tm', split_axis=0, concat_axis=0, tiled=True)  14.5 us
    pallas_call x1, Pallas kernels, per_device(): pl.pallas_call(functools.partial(gather_kernel, devices), out_shape=out_s...  1.69 us

profile of v5, /device:TPU:0, one launch (start us, length us, event | category | flops | bytes accessed | tf_op | source)
XLA Modules:
  0.0 37.5 jit_solution(2858474078089266298)
XLA Ops:
  0.6 20.7 %block_moments.1 = f32[144,128]{1,0:T(8,128)} custom-call(s32[3,8]{1,0:T(4,128)} %bitcast.8, bf16[8,48,12032]{2,1,0:T(8,128)(2,1)} %strain.1, bf16[256,256]{1,0:T(8,128)(2,1)} %constant.2.clone.table, bf16[48,2048]{1,0:T(8,128)(2,1)} %bitcast.7), custom_call_target="tpu_custom_call" | custom-call | tf_op jit(solution)/shard_map/block_moments/pallas_call | solution.py:192
  21.3 14.5 %all_to_all.5 = f32[16,1,1152]{2,1,0:T(1,128)} all-to-all(f32[16,1,1152]{2,1,0:T(1,128)} %bitcast.5), channel_id=1, replica_groups=mesh['groups'=2,'tm'=16] {'tm'}, dimensions={0} | all-to-all | bytes 147456 | tf_op jit(solution)/shard_map/all_to_all | solution.py:281
  35.8 1.7 %gather_damage.1 = (f32[128,128]{1,0:T(8,128)}, f32[1,128]{1,0:T(1,128)}) custom-call(f32[144,128]{1,0:T(8,128)} %bitcast.6), custom_call_target="tpu_custom_call" | custom-call | tf_op jit(solution)/shard_map/gather_damage/pallas_call | solution.py:282

commit v6 on v5

--- a/solution.py
+++ b/solution.py
@@ -21,7 +21,6 @@
 NMOM = 4
 WINDOWS = 96
 STRIDE = 49
-XSHARE = 0
 GROUP = 2
 NT = (((1,), (1,)), ((), ()))
 
@@ -108,7 +107,7 @@
     lane = lax.broadcasted_iota(jnp.int32, (1, LANES), 1)
     keep_odd = lane < tiles - 1
 
-    def work(source, target):
+    def work(source, target, index=0):
         totals = [jnp.zeros((channels, 2 * channels), jnp.float32)] * NMOM
         done = 0
 
@@ -120,15 +119,14 @@
 
         if target is not None:
             for tile in range(tiles):
-                spread_samples(strain, xs, tile)
-                catch_up((tile + 1) * XSHARE // tiles)
+                spread_samples(strain.at[index : index + 1], xs, tile)
             for pair in range(pairs):
                 transform(table, xs, *slots[target], pair)
-                catch_up(XSHARE + (pair + 1) * (lines - XSHARE) // pairs)
+                catch_up((pair + 1) * lines // pairs)
         catch_up(lines)
         if source is None:
             return
-        block = step_index - 1
+        block = 2 * step_index + index - 1
         for moment in range(NMOM):
             whole = (totals[moment][:, :channels] + totals[moment][:, channels:]) * (1.0 / SEGLEN)
             gap = jnp.zeros((channels, CPAD - channels), jnp.float32)
@@ -143,17 +141,17 @@
         weights[...] = jnp.zeros_like(weights)
         for part in range(3):
             weights[part * CPAD : part * CPAD + channels, :] = influence[...]
-        work(None, 0)
-
-    for parity in range(2):
-
-        @pl.when((step_index > 0) & (step_index < blocks) & (step_index % 2 == parity))
-        def _():
-            work(1 - parity, parity)
-
-    @pl.when(step_index == blocks)
+        work(None, 0, 0)
+        work(0, 1, 1)
+
+    @pl.when((step_index > 0) & (step_index < blocks // 2))
     def _():
-        work((blocks - 1) % 2, None)
+        work(1, 0, 0)
+        work(0, 1, 1)
+
+    @pl.when(step_index == blocks // 2)
+    def _():
+        work(1, None, 0)
         width = 2 * LANES
         count = hotspots // width
         part = out.shape[0] // (hotspots // LANES)
@@ -191,10 +189,10 @@
     rows = ((1 if damages else NMOM) * blocks + 1) * (hotspots // LANES)
     return pl.pallas_call(
         functools.partial(moments_kernel, blocks, channels, tiles, damages),
-        grid=(blocks + 1,),
+        grid=(blocks // 2 + 1,),
         in_specs=[
             pl.BlockSpec(memory_space=pltpu.SMEM),
-            pl.BlockSpec((1, channels, samples), lambda b: (jnp.minimum(b, blocks - 1), 0, 0)),
+            pl.BlockSpec((2, channels, samples), lambda b: (jnp.minimum(b, blocks // 2 - 1), 0, 0)),
             pl.BlockSpec((2 * SEGLEN, 2 * SEGLEN), lambda b: (0, 0)),
             pl.BlockSpec((channels, hotspots), lambda b: (0, 0)),
         ],

time: 37.8 us -> 37 us (0.979)
  Pallas kernels: 22.4 us -> 21.6 us
    pallas_call x1, Pallas kernels: 20.7 us -> 19.9 us  [local_rows(): pl.pallas_call(functools.partial(moments_kernel, blocks, channels, tiles,...]
where the time goes in v6:
time: 37 us; the launch traced here: 36.8 us
  Pallas kernels  21.6 us (58%)
  blocking collectives  14.5 us (39%)
  between operations  0.63 us (2%)
    pallas_call x1, Pallas kernels, local_rows(): pl.pallas_call(functools.partial(moments_kernel, blocks, channels, tiles,...  19.9 us
    all_to_all x1, blocking collectives, per_device(): lax.all_to_all(rows, 'tm', split_axis=0, concat_axis=0, tiled=True)  14.5 us
    pallas_call x1, Pallas kernels, per_device(): pl.pallas_call(functools.partial(gather_kernel, devices), out_shape=out_s...  1.69 us

profile of v6, /device:TPU:0, one launch (start us, length us, event | category | flops | bytes accessed | tf_op | source)
XLA Modules:
  0.0 36.8 jit_solution(3234238639018001505)
XLA Ops:
  0.6 19.9 %block_moments.1 = f32[144,128]{1,0:T(8,128)} custom-call(s32[3,8]{1,0:T(4,128)} %bitcast.8, bf16[8,48,12032]{2,1,0:T(8,128)(2,1)} %strain.1, bf16[256,256]{1,0:T(8,128)(2,1)} %constant.2.clone.table, bf16[48,2048]{1,0:T(8,128)(2,1)} %bitcast.7), custom_call_target="tpu_custom_call" | custom-call | tf_op jit(solution)/shard_map/block_moments/pallas_call | solution.py:190
  20.6 14.5 %all_to_all.5 = f32[16,1,1152]{2,1,0:T(1,128)} all-to-all(f32[16,1,1152]{2,1,0:T(1,128)} %bitcast.5), channel_id=1, replica_groups=mesh['groups'=2,'tm'=16] {'tm'}, dimensions={0} | all-to-all | bytes 147456 | tf_op jit(solution)/shard_map/all_to_all | solution.py:279
  35.1 1.7 %gather_damage.1 = (f32[128,128]{1,0:T(8,128)}, f32[1,128]{1,0:T(1,128)}) custom-call(f32[144,128]{1,0:T(8,128)} %bitcast.6), custom_call_target="tpu_custom_call" | custom-call | tf_op jit(solution)/shard_map/gather_damage/pallas_call | solution.py:280

commit v7 on v6

--- a/solution.py
+++ b/solution.py
@@ -144,14 +144,14 @@
         work(None, 0, 0)
         work(0, 1, 1)
 
-    @pl.when((step_index > 0) & (step_index < blocks // 2))
+    @pl.when(step_index > 0)
     def _():
         work(1, 0, 0)
         work(0, 1, 1)
 
-    @pl.when(step_index == blocks // 2)
+    @pl.when(step_index == blocks // 2 - 1)
     def _():
-        work(1, None, 0)
+        work(1, None, 2)
         width = 2 * LANES
         count = hotspots // width
         part = out.shape[0] // (hotspots // LANES)
@@ -189,10 +189,10 @@
     rows = ((1 if damages else NMOM) * blocks + 1) * (hotspots // LANES)
     return pl.pallas_call(
         functools.partial(moments_kernel, blocks, channels, tiles, damages),
-        grid=(blocks // 2 + 1,),
+        grid=(blocks // 2,),
         in_specs=[
             pl.BlockSpec(memory_space=pltpu.SMEM),
-            pl.BlockSpec((2, channels, samples), lambda b: (jnp.minimum(b, blocks // 2 - 1), 0, 0)),
+            pl.BlockSpec((2, channels, samples), lambda b: (b, 0, 0)),
             pl.BlockSpec((2 * SEGLEN, 2 * SEGLEN), lambda b: (0, 0)),
             pl.BlockSpec((channels, hotspots), lambda b: (0, 0)),
         ],

time: 37 us -> 36.9 us (level)
  no operation moved by 1% of the time
where the time goes in v7:
time: 36.9 us; the launch traced here: 36.7 us
  Pallas kernels  21.6 us (59%)
  blocking collectives  14.5 us (39%)
  between operations  0.63 us (2%)
    pallas_call x1, Pallas kernels, local_rows(): pl.pallas_call(functools.partial(moments_kernel, blocks, channels, tiles,...  19.9 us
    all_to_all x1, blocking collectives, per_device(): lax.all_to_all(rows, 'tm', split_axis=0, concat_axis=0, tiled=True)  14.5 us
    pallas_call x1, Pallas kernels, per_device(): pl.pallas_call(functools.partial(gather_kernel, devices), out_shape=out_s...  1.69 us

profile of v7, /device:TPU:0, one launch (start us, length us, event | category | flops | bytes accessed | tf_op | source)
XLA Modules:
  0.0 36.7 jit_solution(9148506760943034302)
XLA Ops:
  0.6 19.9 %block_moments.1 = f32[144,128]{1,0:T(8,128)} custom-call(s32[3,8]{1,0:T(4,128)} %bitcast.8, bf16[8,48,12032]{2,1,0:T(8,128)(2,1)} %strain.1, bf16[256,256]{1,0:T(8,128)(2,1)} %constant.2.clone.table, bf16[48,2048]{1,0:T(8,128)(2,1)} %bitcast.7), custom_call_target="tpu_custom_call" | custom-call | tf_op jit(solution)/shard_map/block_moments/pallas_call | solution.py:190
  20.5 14.5 %all_to_all.5 = f32[16,1,1152]{2,1,0:T(1,128)} all-to-all(f32[16,1,1152]{2,1,0:T(1,128)} %bitcast.5), channel_id=1, replica_groups=mesh['groups'=2,'tm'=16] {'tm'}, dimensions={0} | all-to-all | bytes 147456 | tf_op jit(solution)/shard_map/all_to_all | solution.py:279
  35.0 1.7 %gather_damage.1 = (f32[128,128]{1,0:T(8,128)}, f32[1,128]{1,0:T(1,128)}) custom-call(f32[144,128]{1,0:T(8,128)} %bitcast.6), custom_call_target="tpu_custom_call" | custom-call | tf_op jit(solution)/shard_map/gather_damage/pallas_call | solution.py:280
